TPU v7x, 256 devices: a whole 4x4x8 slice. The times are simulated.
256 devices in a mesh: sec: 4 (over z_lo), band: 32 (over y, z_hi, x), ch: 2 (over core).
Axes of the slice: x: 4, y: 4, z: 8 (z_hi: 2, z_lo: 4; z = z_hi * 4 + z_lo), core: 2. Of those that a mesh axis runs over, the one named last changes fastest.
Arguments:
- air_field_lattice: bfloat16 [512, 1024, 768], P(('sec', 'band', 'ch')), may hold values from -6 to 6
- associated_polynomial_matrix: bfloat16 [512, 512, 512], P(('sec', 'band', 'ch')), may hold values from -0.25 to 0.25
- harmonic_damping_factor: float32 [512, 768], replicated, may hold values from 0.5 to 2
- boundary_exchange_projector: bfloat16 [768, 8], replicated, may hold values from -0.21875 to 0.21875
- warmth_response_factor: float32 [768], replicated, may hold values from -4 to 4
- water_patch_fields: bfloat16 [1536, 128, 4, 258], P(('sec', 'band', 'ch')), may hold values from -6 to 6
- kernel_coefficients: bfloat16 [3, 3, 128, 128], replicated, may hold values from -0.1875 to 0.1875
- local_exchange_matrix: bfloat16 [8, 128], replicated, may hold values from -2 to 2
- patch_average_matrix: float32 [8, 128], replicated, may hold values from -15 to 15
- water_kernel_offset: float32 [128], replicated, may hold values from -3 to 3
- water_readout_matrix: bfloat16 [128, 128], replicated, may hold values from -0.5 to 0.5
- patch_holder_index: int32 [256, 4], replicated, may hold values from 0 to 31, as said below
- water_point_indicator: int32 [1536, 2, 256], P(('sec', 'band', 'ch')), may hold values from 0 to 1, as said below
- water_point_totals: int32 [1536], P(('sec', 'band', 'ch')), may hold values from 0 to 512, as said below
Outputs:
- advanced_air_field: bfloat16 [512, 1024, 768], P(('sec', 'band', 'ch'))
- ocean_next: bfloat16 [1536, 128, 2, 256], P(('sec', 'band', 'ch'))
Inputs may be any that keep to these rules, and one draw needn't show every extreme that they name: `patch_holder_index`: within each group of equal s and c, every band index owns either 6 or 2 of the group's tiles, half of them each way, so no device owns more than 6. `water_point_indicator`: empty slots are all zeros. `water_point_totals`: the number of ones of the slot in water_point_indicator.
All inputs are finite; a program needn't handle non-finite values.
Results may differ from a plain program's by a relative error of at most 0.0058.
Values may be sent and summed in bfloat16 or wider, within the bound.
A program may use at most 128 MiB of HBM per device.

v0:
```python
import math

import jax
import jax.numpy as jnp
from jax import lax
from jax.sharding import PartitionSpec as P

K = 512


def dft_tables(meridian_number, column_order):
    cell_index = jnp.arange(meridian_number, dtype=jnp.int32)[:, None]
    wavenumber = (column_order // 2)[None, :]
    component = (column_order % 2)[None, :]
    phase_angle = (cell_index * wavenumber % meridian_number).astype(jnp.float32) * (
        2.0 * math.pi / meridian_number
    )
    basis_table = jnp.where(component == 0, jnp.cos(phase_angle), -jnp.sin(phase_angle))
    forward = basis_table.astype(jnp.bfloat16)
    inverse = (basis_table.T * (2.0 / meridian_number)).astype(jnp.bfloat16)
    return (forward, inverse)


def ocean_update(
    state,
    tile_flux,
    mask_tile,
    count_tile,
    kernel_coefficients,
    local_exchange_matrix,
    patch_average_matrix,
    water_kernel_offset,
    water_readout_matrix,
):
    parallel_lines = mask_tile.shape[1]
    tile_width = mask_tile.shape[2]
    mask_f = mask_tile.astype(jnp.float32)
    masked = tile_flux * mask_tile[:, None].astype(jnp.bfloat16)
    fmean = (
        jnp.sum(masked.astype(jnp.float32), axis=(2, 3))
        / jnp.maximum(count_tile.astype(jnp.float32), 1.0)[:, None]
    )
    total = jnp.einsum(
        "fo,sfrw->sorw", local_exchange_matrix, masked, preferred_element_type=jnp.float32
    )
    for shift_row in range(3):
        for shift_col in range(3):
            window = state[
                :, :, shift_row : shift_row + parallel_lines, shift_col : shift_col + tile_width
            ]
            total = total + jnp.einsum(
                "io,sirw->sorw",
                kernel_coefficients[shift_row, shift_col],
                window,
                preferred_element_type=jnp.float32,
            )
    mean_term = jnp.sum(fmean[:, :, None] * patch_average_matrix[None], axis=1)
    total = total + mean_term[:, :, None, None] + water_kernel_offset[None, :, None, None]
    hidden = jax.nn.gelu(total, approximate=True).astype(jnp.bfloat16)
    update = jnp.einsum(
        "io,sirw->sorw", water_readout_matrix, hidden, preferred_element_type=jnp.float32
    )
    fresh = (
        state[:, :, 1 : 1 + parallel_lines, 1 : 1 + tile_width].astype(jnp.float32) + update
    ) * mask_f[:, None]
    return fresh.astype(jnp.bfloat16)


def shards(
    air_field_lattice,
    associated_polynomial_matrix,
    harmonic_damping_factor,
    boundary_exchange_projector,
    warmth_response_factor,
    water_patch_fields,
    kernel_coefficients,
    local_exchange_matrix,
    patch_average_matrix,
    water_kernel_offset,
    water_readout_matrix,
    patch_holder_index,
    water_point_indicator,
    water_point_totals,
):
    parallel_lines, meridian_number, channel_count = air_field_lattice.shape
    sec_count = lax.axis_size("sec")
    band_count = lax.axis_size("band")
    core_count = lax.axis_size("ch")
    device_count = sec_count * band_count * core_count
    total_cols = 2 * K
    per_device = total_cols // device_count
    slot_count = water_patch_fields.shape[0]
    flux_local = jnp.einsum(
        "anc,cf->fan",
        air_field_lattice,
        boundary_exchange_projector,
        preferred_element_type=jnp.float32,
    ).astype(jnp.bfloat16)
    gathered = lax.all_gather(flux_local, "band", axis=1, tiled=True)
    sec_id = lax.axis_index("sec")
    band_id = lax.axis_index("band")
    core_id = lax.axis_index("ch")
    owner_grid = patch_holder_index.reshape(sec_count, band_count, core_count, -1)
    tiles_per_row = owner_grid.shape[3]
    owner_group = lax.dynamic_index_in_dim(owner_grid, sec_id, 0, keepdims=False)
    owner_group = lax.dynamic_index_in_dim(owner_group, core_id, 1, keepdims=False)
    owner_flat = owner_group.reshape(-1)
    holders = jnp.arange(band_count, dtype=jnp.int32)
    mine_all = owner_flat[None, :] == holders[:, None]
    rank_all = jnp.cumsum(mine_all.astype(jnp.int32), axis=1) - 1
    slot_index = jnp.arange(slot_count, dtype=jnp.int32)
    pick_all = mine_all[:, None, :] & (rank_all[:, None, :] == slot_index[None, :, None])
    my_pick = lax.dynamic_index_in_dim(pick_all, band_id, 0, keepdims=False)
    flux_count = gathered.shape[0]
    tile_width = meridian_number // tiles_per_row
    pieces = gathered.reshape(flux_count, band_count, parallel_lines, tiles_per_row, tile_width)
    chooser = my_pick.reshape(slot_count, band_count, tiles_per_row).astype(jnp.bfloat16)
    tile_flux = jnp.einsum(
        "sbj,fbrjw->sfrw", chooser, pieces, preferred_element_type=jnp.float32
    ).astype(jnp.bfloat16)
    ocean_next = ocean_update(
        water_patch_fields,
        tile_flux,
        water_point_indicator,
        water_point_totals,
        kernel_coefficients,
        local_exchange_matrix,
        patch_average_matrix,
        water_kernel_offset,
        water_readout_matrix,
    )
    sea_slots = ocean_next[:, 0]
    sea_all = lax.all_gather(sea_slots, "band", axis=0, tiled=True)
    rank_tile = jnp.sum(jnp.where(mine_all, rank_all, 0), axis=0)
    my_owners = lax.dynamic_index_in_dim(owner_group, band_id, 0, keepdims=False)
    my_ranks = lax.dynamic_slice_in_dim(rank_tile, band_id * tiles_per_row, tiles_per_row)
    target = my_owners * slot_count + my_ranks
    selector = (
        target[:, None] == jnp.arange(band_count * slot_count, dtype=jnp.int32)[None, :]
    ).astype(jnp.bfloat16)
    water_patches = jnp.einsum(
        "jk,krw->rjw", selector, sea_all, preferred_element_type=jnp.float32
    ).astype(jnp.bfloat16)
    water_skin_warmth = water_patches.reshape(parallel_lines, meridian_number)
    mode_count = associated_polynomial_matrix.shape[0]
    lat_count = associated_polynomial_matrix.shape[1]
    sb_count = sec_count * band_count
    column_order = jnp.arange(total_cols, dtype=jnp.int32)
    forward, inverse = dft_tables(meridian_number, column_order)
    fourier = jnp.einsum(
        "nq,anc->qac", forward, air_field_lattice, preferred_element_type=jnp.float32
    ).astype(jnp.bfloat16)
    collected = lax.all_to_all(
        lax.all_to_all(fourier, ("sec", "band"), split_axis=0, concat_axis=1, tiled=True),
        "ch",
        split_axis=0,
        concat_axis=1,
        tiled=True,
    )
    transform_local = associated_polynomial_matrix.reshape(
        mode_count, lat_count, sb_count, core_count, parallel_lines
    )
    transform_local = transform_local.transpose(0, 1, 3, 2, 4).reshape(
        mode_count, lat_count, lat_count
    )
    coeff_pairs = collected.reshape(mode_count, 2, lat_count, channel_count)
    spectrum = jnp.einsum(
        "mlt,mptc->mplc", transform_local, coeff_pairs, preferred_element_type=jnp.float32
    )
    scaled = (spectrum * harmonic_damping_factor[None, None]).astype(jnp.bfloat16)
    damped_modes = jnp.einsum(
        "mlt,mplc->mptc", transform_local, scaled, preferred_element_type=jnp.float32
    )
    damped_modes = damped_modes.astype(jnp.bfloat16).reshape(per_device, lat_count, channel_count)
    returned = lax.all_to_all(
        lax.all_to_all(damped_modes, "ch", split_axis=1, concat_axis=0, tiled=True),
        ("sec", "band"),
        split_axis=1,
        concat_axis=0,
        tiled=True,
    )
    reconstruct_physical = jnp.einsum(
        "qn,qac->anc", inverse, returned, preferred_element_type=jnp.float32
    )
    advanced_pair = (
        air_field_lattice.astype(jnp.float32)
        + reconstruct_physical
        + water_skin_warmth.astype(jnp.float32)[:, :, None] * warmth_response_factor[None, None, :]
    )
    return (advanced_pair.astype(jnp.bfloat16), ocean_next)


def solution(mesh):
    placed = (
        P(("sec", "band", "ch"), None, None),
        P(("sec", "band", "ch"), None, None),
        P(),
        P(),
        P(),
        P(("sec", "band", "ch"), None, None, None),
        P(),
        P(),
        P(),
        P(),
        P(),
        P(),
        P(("sec", "band", "ch"), None, None),
        P(("sec", "band", "ch")),
    )
    return jax.shard_map(
        shards,
        mesh=mesh,
        in_specs=placed,
        out_specs=(
            P(("sec", "band", "ch"), None, None),
            P(("sec", "band", "ch"), None, None, None),
        ),
        check_vma=False,
    )
```

profile of v0, /device:TPU:32, one launch (start us, length us, event | category | flops | bytes accessed | tf_op | source)
XLA Modules:
  0.0 381.3 jit_solution(11099268544566484406)
XLA Ops:
  8.4 21.6 %convolution_convert_fusion = bf16[1024,2,768]{2,0,1:T(8,128)(2,1)S(1)} fusion(bf16[2,1024,768]{2,1,0:T(8,128)(2,1)} %param.14, s32[1024]{0:T(1024)S(1)} %add_select_fusion.2, pred[1024]{0:T(1024)(128)(4,1)S(1)} %fusion.111), kind=kOutput, calls=%fused_computation.33 | convolution fusion | flops 3240624128 | bytes 6296576 | tf_op jit(solution)/shard_map/nq,anc->qac/dot_general | solution.py:150
  30.0 4.9 %copy.187 = bf16[1024,2,768]{2,1,0:T(2,128)(2,1)} copy(bf16[1024,2,768]{2,0,1:T(8,128)(2,1)S(1)} %convolution_convert_fusion) | data formatting | bytes 6291456 | tf_op jit(solution)/shard_map/convert_element_type | solution.py:152
  34.9 15.8 %all-to-all-start = ((bf16[1024,2,768]{2,1,0:T(2,128)(2,1)}), bf16[1024,2,768]{2,1,0:T(2,128)(2,1)}, u32[]{:S(2)}, u32[]{:S(2)}) async-start(bf16[1024,2,768]{2,1,0:T(2,128)(2,1)} %copy.187), calls=%async_computation | async-start | bytes 6291456 | tf_op jit(solution)/shard_map/all_to_all | solution.py:154
  53.0 2.5 copy.192
  56.2 2.5 copy.229
  58.7 3.0 copy.196
  61.8 64.7 %all-to-all-done = bf16[1024,2,768]{2,1,0:T(2,128)(2,1)} async-done(((bf16[1024,2,768]{2,1,0:T(2,128)(2,1)}), bf16[1024,2,768]{2,1,0:T(2,128)(2,1)}, u32[]{:S(2)}, u32[]{:S(2)}) %all-to-all-start) | async-done | bytes 3145760 | tf_op jit(solution)/shard_map/all_to_all | solution.py:154
  126.5 2.3 copy.305
  129.6 6.5 %all_to_all.69 = bf16[8,256,768]{2,1,0:T(8,128)(2,1)S(1)} all-to-all(bf16[8,256,768]{2,1,0:T(8,128)(2,1)S(1)} %copy.190), channel_id=1, replica_groups=mesh['sec'=4,'band'=32,'ch'=2] {'ch'}, dimensions={0} | all-to-all | bytes 6291456 | tf_op jit(solution)/shard_map/all_to_all | solution.py:153
  136.3 7.2 %fusion.23 = bf16[2,2,768,512]{3,2,1,0:T(8,128)(2,1)} fusion(bf16[2,512,512,1]{2,1,3,0:T(8,128)(2,1)} %copy.229, f32[512,768]{0,1:T(8,128)} %copy.196, bf16[2,2,512,768]{3,2,1,0:T(8,128)(2,1)S(1)} %bitcast.182), kind=kOutput, calls=%fused_computation.34 | convolution fusion | flops 3225944064 | bytes 8912896 | tf_op jit(solution)/shard_map/mlt,mplc->mptc/dot_general | solution.py:171
  143.5 4.7 %copy.198 = bf16[4,512,768]{2,0,1:T(4,128)(2,1)S(1)} copy(bf16[4,512,768]{1,2,0:T(8,128)(2,1)} %bitcast.183) | data formatting | bytes 6291456 | tf_op jit(solution)/shard_map/reshape | solution.py:174
  148.2 6.3 %all_to_all.70 = bf16[4,512,768]{2,0,1:T(4,128)(2,1)S(1)} all-to-all(bf16[4,512,768]{2,0,1:T(4,128)(2,1)S(1)} %copy.198), channel_id=1, replica_groups=mesh['sec'=4,'band'=32,'ch'=2] {'ch'}, dimensions={1} | all-to-all | bytes 6291456 | tf_op jit(solution)/shard_map/all_to_all | solution.py:176
  155.1 3.4 copy.201
  158.5 17.9 %all-to-all-start.3 = ((bf16[8,256,768]{2,0,1:T(8,128)(2,1)}), bf16[8,256,768]{2,0,1:T(8,128)(2,1)}, u32[]{:S(2)}, u32[]{:S(2)}) async-start(bf16[8,256,768]{2,0,1:T(8,128)(2,1)} %copy.201), calls=%async_computation.3 | async-start | bytes 6291456 | tf_op jit(solution)/shard_map/all_to_all | solution.py:175
  177.1 8.5 %fusion.139 = (bf16[6,128,2,256]{1,2,3,0:T(2,128)(2,1)}, bf16[6,128,2,256]{1,2,3,0:T(2,128)(2,1)}, bf16[6,128,2,256]{1,2,3,0:T(2,128)(2,1)}, bf16[6,128,2,256]{1...) fusion(bf16[6,128,4,258]{1,2,3,0:T(4,128)(2,1)S(1)} %copy-done.1), kind=kLoop, calls=%fused_computation.161 | loop fusion | bytes 14155776 | tf_op jit(solution)/shard_map/slice | solution.py:48
  190.9 2.9 copy.185
  195.2 2.7 fusion.64
  198.0 2.7 fusion.66
  208.4 1.9 reshape.144
  212.6 6.3 %fusion.52 = bf16[6,128,2,256]{1,3,2,0:T(8,128)(2,1)S(1)} fusion(f32[6,2,256,128]{3,2,1,0:T(8,128)} %fusion.62, f32[6,2,256,128]{3,2,1,0:T(8,128)} %fusion.64, f32[6,2,256,128]{3,2,1,0:T(8,128)} %fusion.66, f32[6,2,256,128]{3,2,1,0:T(8,128)} %fusion.68, f32[6,2,256,128]{3,2,1,0:T(8,128)S(1)} %copy-done.6, f32[6,2,256,128]{3,2,1,0:T(8,128)} %fusion.70, ...), kind=kOutput, calls=%fused_computation.60 | convolution fusion | flops 116391936 | bytes 15828480 | tf_op jit(solution)/shard_map/io,sirw->sorw/dot_general | solution.py:60
  218.8 1.8 copy.226
  220.9 127.4 %all-gather = bf16[192,1,2,256]{3,2,1,0:T(2,128)(2,1)S(1)} all-gather(bf16[6,1,2,256]{3,2,1,0:T(2,128)(2,1)S(1)} %copy.223), channel_id=2, replica_groups=mesh['sec'=4,'band'=32,'ch'=2] {'band'}, dimensions={0}, use_global_device_ids=true | all-gather | bytes 202752 | tf_op jit(solution)/shard_map/all_gather | solution.py:133
  348.5 22.9 %fusion.1 = bf16[2,1024,768]{1,2,0:T(8,128)(2,1)S(1)} fusion(bf16[2,1024,768]{1,2,0:T(8,128)(2,1)} %copy.185, f32[768]{0:T(1024)S(1)} %copy-done.21, f32[2,1024]{1,0:T(2,128)S(1)} %bitcast.187, s32[1024]{0:T(1024)S(1)} %copy-done.19, pred[1024]{0:T(1024)(128)(4,1)S(1)} %copy-done.24, bf16[128,8,2,768]{3,1,2,0:T(8,128)(2,1)} %bitcast.19), kind=kOutput, calls=%fused_computation.2 | convolution fusion | flops 3247964160 | bytes 9453568 | tf_op jit(solution)/shard_map/qn,qac->anc/dot_general | solution.py:182
  371.5 2.8 copy.225
  (92 shorter events, 23.7 us)
Async XLA Ops:
  7.2 205.3 %copy-start = (bf16[128,128]{1,0:T(8,128)(2,1)S(1)}, bf16[128,128]{1,0:T(8,128)(2,1)}, u32[]{:S(2)}) copy-start(bf16[128,128]{1,0:T(8,128)(2,1)} %param.24) | copy-start | bytes 98308
  34.9 15.8 %copy-start.2 = (bf16[2,1024,768]{2,1,0:T(8,128)(2,1)S(1)}, bf16[2,1024,768]{2,1,0:T(8,128)(2,1)}, u32[]{:S(2)}) copy-start(bf16[2,1024,768]{2,1,0:T(8,128)(2,1)} %param.14) | copy-start | bytes 9437188
  34.9 15.8 %copy-start.14 = (bf16[768,8]{0,1:T(8,128)(2,1)S(1)}, bf16[768,8]{0,1:T(8,128)(2,1)}, u32[]{:S(2)}) copy-start(bf16[768,8]{0,1:T(8,128)(2,1)} %param.17) | copy-start | bytes 36868
  34.9 91.6 %all-to-all-start = ((bf16[1024,2,768]{2,1,0:T(2,128)(2,1)}), bf16[1024,2,768]{2,1,0:T(2,128)(2,1)}, u32[]{:S(2)}, u32[]{:S(2)}) async-start(bf16[1024,2,768]{2,1,0:T(2,128)(2,1)} %copy.187), calls=%async_computation | async-start | bytes 6291456 | tf_op jit(solution)/shard_map/all_to_all | solution.py:154
  50.7 157.7 %all-gather.3.cloned.1.call-start = ((), (), s32[]{:S(2)}) async-start(), calls=%async_computation.4 | async-start | bytes 1081344 | tf_op jit(solution)/shard_map/all_gather | solution.py:99
  52.5 3.0 copy-start.13
  158.5 18.0 %copy-start.22 = (s32[6]{0:T(128)S(1)}, s32[6]{0:T(128)}, u32[]{:S(2)}) copy-start(s32[6]{0:T(128)} %param.27) | copy-start | bytes 76
  158.5 18.5 %copy-start.15 = (s32[6,2,256]{2,1,0:T(2,128)S(1)}, s32[6,2,256]{2,1,0:T(2,128)}, u32[]{:S(2)}) copy-start(s32[6,2,256]{2,1,0:T(2,128)} %param.26) | copy-start | bytes 36868
  158.5 18.5 %copy-start.1 = (bf16[6,128,4,258]{1,2,3,0:T(4,128)(2,1)S(1)}, bf16[6,128,4,258]{1,2,3,0:T(4,128)(2,1)}, u32[]{:S(2)}) copy-start(bf16[6,128,4,258]{1,2,3,0:T(4,128)(2,1)} %param.19) | copy-start | bytes 4755460
  158.5 190.0 %all-to-all-start.3 = ((bf16[8,256,768]{2,0,1:T(8,128)(2,1)}), bf16[8,256,768]{2,0,1:T(8,128)(2,1)}, u32[]{:S(2)}, u32[]{:S(2)}) async-start(bf16[8,256,768]{2,0,1:T(8,128)(2,1)} %copy.201), calls=%async_computation.3 | async-start | bytes 6291456 | tf_op jit(solution)/shard_map/all_to_all | solution.py:175
  177.1 9.4 %copy-start.12 = (bf16[3,3,128,128]{3,2,1,0:T(8,128)(2,1)S(1)}, bf16[3,3,128,128]{3,2,1,0:T(8,128)(2,1)}, u32[]{:S(2)}) copy-start(bf16[3,3,128,128]{3,2,1,0:T(8,128)(2,1)} %param.20) | copy-start | bytes 884740
  185.6 5.3 %copy-start.3 = (bf16[2,1024,768]{2,1,0:T(8,128)(2,1)S(1)}, bf16[2,1024,768]{2,1,0:T(8,128)(2,1)}, u32[]{:S(2)}) copy-start(bf16[2,1024,768]{2,1,0:T(8,128)(2,1)} %param.14) | copy-start | bytes 9437188
  193.8 6.9 %copy-start.11 = (bf16[6,128,2,256]{1,2,3,0:T(2,128)(2,1)S(1)}, bf16[6,128,2,256]{1,2,3,0:T(2,128)(2,1)}, u32[]{:S(2)}) copy-start(bf16[6,128,2,256]{1,2,3,0:T(2,128)(2,1)} %get-tuple-element.17) | copy-start | bytes 2359300
  195.2 7.0 %copy-start.10 = (bf16[6,128,2,256]{1,2,3,0:T(2,128)(2,1)S(1)}, bf16[6,128,2,256]{1,2,3,0:T(2,128)(2,1)}, u32[]{:S(2)}) copy-start(bf16[6,128,2,256]{1,2,3,0:T(2,128)(2,1)} %get-tuple-element.18) | copy-start | bytes 2359300
  198.0 5.8 %copy-start.9 = (bf16[6,128,2,256]{1,2,3,0:T(2,128)(2,1)S(1)}, bf16[6,128,2,256]{1,2,3,0:T(2,128)(2,1)}, u32[]{:S(2)}) copy-start(bf16[6,128,2,256]{1,2,3,0:T(2,128)(2,1)} %get-tuple-element.19) | copy-start | bytes 2359300
  200.7 4.6 %copy-start.8 = (bf16[6,128,2,256]{1,2,3,0:T(2,128)(2,1)S(1)}, bf16[6,128,2,256]{1,2,3,0:T(2,128)(2,1)}, u32[]{:S(2)}) copy-start(bf16[6,128,2,256]{1,2,3,0:T(2,128)(2,1)} %get-tuple-element.20) | copy-start | bytes 2359300
  202.2 4.6 %copy-start.7 = (bf16[6,128,2,256]{1,2,3,0:T(2,128)(2,1)S(1)}, bf16[6,128,2,256]{1,2,3,0:T(2,128)(2,1)}, u32[]{:S(2)}) copy-start(bf16[6,128,2,256]{1,2,3,0:T(2,128)(2,1)} %get-tuple-element.14) | copy-start | bytes 2359300
  206.8 5.6 %copy-start.17 = (f32[8,128]{1,0:T(8,128)S(1)}, f32[8,128]{1,0:T(8,128)}, u32[]{:S(2)}) copy-start(f32[8,128]{1,0:T(8,128)} %param.22) | copy-start | bytes 12292
  206.8 5.7 %copy-start.5 = (bf16[6,128,2,256]{1,2,3,0:T(2,128)(2,1)S(1)}, bf16[6,128,2,256]{1,2,3,0:T(2,128)(2,1)}, u32[]{:S(2)}) copy-start(bf16[6,128,2,256]{1,2,3,0:T(2,128)(2,1)} %copy-done.4) | copy-start | bytes 2359300
  206.8 5.7 %copy-start.6 = (f32[6,2,256,128]{3,2,1,0:T(8,128)S(1)}, f32[6,2,256,128]{3,2,1,0:T(8,128)}, u32[]{:S(2)}) copy-start(f32[6,2,256,128]{3,2,1,0:T(8,128)} %fusion.84) | copy-start | bytes 4718596
  212.5 135.8 %copy-start.20 = (s32[4]{0:T(128)S(1)}, s32[4]{0:T(128)}, u32[]{:S(2)}) copy-start(s32[4]{0:T(128)} %fusion.127) | copy-start | bytes 52
  212.5 136.0 %copy-start.19 = (s32[1024]{0:T(1024)S(1)}, s32[1024]{0:T(1024)}, u32[]{:S(2)}) copy-start(s32[1024]{0:T(1024)} %copy-done.18) | copy-start | bytes 12292
  212.6 136.0 %copy-start.21 = (f32[768]{0:T(1024)S(1)}, f32[768]{0:T(1024)}, u32[]{:S(2)}) copy-start(f32[768]{0:T(1024)} %param.18) | copy-start | bytes 9220
  212.6 136.0 %copy-start.24 = (pred[1024]{0:T(1024)(128)(4,1)S(1)}, pred[1024]{0:T(1024)(128)(4,1)}, u32[]{:S(2)}) copy-start(pred[1024]{0:T(1024)(128)(4,1)} %copy-done.23) | copy-start | bytes 3076
  (4 other events, 3.7 us)
Sparse Core Ops, SparseCore 0:
  54.9 86.5 all-gather.2
where the time goes:
time: 389 us; the launch traced here: 381 us
  blocking collectives  140 us (36%)
  matrix products  77.4 us (20%)
  waiting for transfers between devices  64.7 us (17%)
  local copies, waits for them, and re-layouts  47.9 us (12%)
  starting transfers between devices  33.7 us (9%)
  between operations  14.7 us (4%)
    all_gather x1, blocking collectives, shards(): sea_all = lax.all_gather(sea_slots, 'band', axis=0, tiled=True)  127 us
    all_to_all x1, waiting for transfers between devices, shards(): lax.all_to_all(fourier, ('sec', 'band'), split_axis=0, concat_axis=1, til...  64.7 us
    dot_general x1, matrix products, shards(): jnp.einsum('qn,qac->anc', inverse, returned, preferred_element_type=jnp.f...  22.9 us
    dot_general x1, matrix products, shards(): jnp.einsum('nq,anc->qac', forward, air_field_lattice, preferred_element_t...  21.6 us
    all_to_all x1, starting transfers between devices, shards(): lax.all_to_all(lax.all_to_all(damped_modes, 'ch', split_axis=1, concat_ax...  17.9 us
    dot_general x9, matrix products, ocean_update(): jnp.einsum('io,sirw->sorw', kernel_coefficients[shift_row, shift_col], wi...  16.2 us
    all_to_all x1, starting transfers between devices, shards(): lax.all_to_all(fourier, ('sec', 'band'), split_axis=0, concat_axis=1, til...  15.8 us
    unnamed x57, local copies, waits for them, and re-layouts  15.3 us
  transfers between devices with their start and end apart: 3, of which 1 were waited for; matrix products, arithmetic and copies ran while one was open for 19% of the time, Pallas kernels for 0%

commit v1 on v0

--- a/solution.py
+++ b/solution.py
@@ -1,24 +1,361 @@
+import functools
 import math
 
 import jax
 import jax.numpy as jnp
+import numpy as np
 from jax import lax
+from jax.experimental import pallas as pl
+from jax.experimental.pallas import tpu as pltpu
 from jax.sharding import PartitionSpec as P
 
-K = 512
-
-
-def dft_tables(meridian_number, column_order):
-    cell_index = jnp.arange(meridian_number, dtype=jnp.int32)[:, None]
-    wavenumber = (column_order // 2)[None, :]
-    component = (column_order % 2)[None, :]
-    phase_angle = (cell_index * wavenumber % meridian_number).astype(jnp.float32) * (
-        2.0 * math.pi / meridian_number
-    )
-    basis_table = jnp.where(component == 0, jnp.cos(phase_angle), -jnp.sin(phase_angle))
-    forward = basis_table.astype(jnp.bfloat16)
-    inverse = (basis_table.T * (2.0 / meridian_number)).astype(jnp.bfloat16)
-    return (forward, inverse)
+MESH = pl.DeviceIdType.MESH
+CHUNKS = (256, 256, 256)
+NZ, NY, NX, NC = 8, 4, 4, 2
+NP = NY * NX * NC
+N = 1024
+LAT = 512
+
+
+def trig(a, b):
+    phase = (a[:, None].astype(np.int64) * b[None, :]) % N
+    angle = phase.astype(np.float64) * (2.0 * math.pi / N)
+    return np.cos(angle).astype(np.float32), np.sin(angle).astype(np.float32)
+
+
+def basis_tables():
+    n = np.arange(N)
+    zh, zl, part, y = np.meshgrid(np.arange(2), np.arange(4), np.arange(2), np.arange(4), indexing="ij")
+    k_hi = (zl * 128 + y * 32 + zh * 16).reshape(-1)
+    part_hi = part.reshape(-1)[:, None]
+    k_lo = np.arange(16)
+    ch, sh = trig(k_hi, n)
+    cl, sl = trig(k_lo, n)
+    u1 = np.where(part_hi == 0, ch, -sh)
+    u2 = np.where(part_hi == 0, -sh, -ch)
+    fwd = jnp.asarray(u1)[:, None, :] * jnp.asarray(cl)[None] + jnp.asarray(u2)[:, None, :] * jnp.asarray(sl)[None]
+    fwd = fwd.astype(jnp.bfloat16).reshape(N, N)
+    k_all = (k_hi[:, None] + k_lo[None, :]).reshape(-1)
+    part_all = np.repeat(part.reshape(-1), 16)[None, :]
+    c1, s1 = trig(np.arange(32) * 32, k_all)
+    c0, s0 = trig(np.arange(32), k_all)
+    v1 = np.where(part_all == 0, c1, -s1)
+    v2 = np.where(part_all == 0, -s1, -c1)
+    inv = jnp.asarray(v1)[:, None, :] * jnp.asarray(c0)[None] + jnp.asarray(v2)[:, None, :] * jnp.asarray(s0)[None]
+    inv = inv.astype(jnp.bfloat16).reshape(N, N)
+    return fwd, inv
+
+
+def one_hot(rows, cols, fn):
+    r = lax.broadcasted_iota(jnp.int32, (rows, cols), 0)
+    c = lax.broadcasted_iota(jnp.int32, (rows, cols), 1)
+    return jnp.where(fn(r, c), 1.0, 0.0).astype(jnp.bfloat16)
+
+
+def true_lat(i):
+    t = i & 1
+    z_lo = (i >> 1) & 3
+    z_hi = (i >> 3) & 1
+    c = (i >> 4) & 1
+    x = (i >> 5) & 3
+    y = (i >> 7) & 3
+    return (z_lo * 64 + y * 16 + z_hi * 8 + x * 2 + c) * 2 + t
+
+
+def spectral_kernel(
+    air_hbm, fwd_hbm, inv_hbm, pol_hbm, damp_hbm, warm_ref, sea_ref, out_hbm, *scr
+):
+    nchunk = len(CHUNKS)
+    it = iter(scr)
+    fwd, inv, pol, polp, polt, damp, q1, q2 = (next(it) for _ in range(8))
+    airv = [next(it) for _ in CHUNKS]
+    zs1 = [next(it) for _ in CHUNKS]
+    zr1 = [next(it) for _ in CHUNKS]
+    ps1 = [next(it) for _ in CHUNKS]
+    mid = [next(it) for _ in CHUNKS]
+    ret = [next(it) for _ in CHUNKS]
+    pr2 = [next(it) for _ in CHUNKS]
+    zs2 = [next(it) for _ in CHUNKS]
+    fin = [next(it) for _ in CHUNKS]
+    load_sem, out_sem, send_sem, recv_sem, self_sem = (next(it) for _ in range(5))
+
+    s = lax.axis_index("sec")
+    b = lax.axis_index("band")
+    c = lax.axis_index("ch")
+    y = b // 8
+    z_hi = lax.rem(b // 4, 2)
+    x = lax.rem(b, 4)
+    z = z_hi * 4 + s
+    p = y * 8 + x * 2 + c
+
+    def z_dev(zz):
+        return (lax.rem(zz, 4), y * 8 + (zz // 4) * 4 + x, c)
+
+    def p_dev(pp):
+        return (s, (pp // 8) * 8 + z_hi * 4 + lax.rem(pp // 2, 4), lax.rem(pp, 2))
+
+    offs = [0]
+    for w in CHUNKS:
+        offs.append(offs[-1] + w)
+
+    loads = []
+
+    def load(src, dst):
+        copy = pltpu.make_async_copy(src, dst, load_sem.at[len(loads)])
+        copy.start()
+        loads.append(copy)
+        return copy
+
+    ld_fwd = load(fwd_hbm, fwd)
+    ld_air = [load(air_hbm.at[:, :, pl.ds(offs[j], CHUNKS[j])], airv[j]) for j in range(nchunk)]
+    ld_pol = load(pol_hbm, pol)
+    ld_damp = load(damp_hbm, damp)
+    ld_inv = load(inv_hbm, inv)
+
+    barrier = pltpu.get_barrier_semaphore()
+
+    def greet_z(i, _):
+        pl.semaphore_signal(barrier, inc=1, device_id=z_dev(lax.rem(z + i, NZ)), device_id_type=MESH)
+        return 0
+
+    def greet_p(i, _):
+        pl.semaphore_signal(barrier, inc=1, device_id=p_dev(lax.rem(p + i, NP)), device_id_type=MESH)
+        return 0
+
+    lax.fori_loop(1, NZ, greet_z, 0)
+    lax.fori_loop(1, NP, greet_p, 0)
+
+    def z_copy(stage, j, src, dst, i):
+        to = lax.rem(z + i, NZ)
+        return pltpu.make_async_remote_copy(
+            src_ref=src.at[to], dst_ref=dst.at[z],
+            send_sem=send_sem.at[stage, j], recv_sem=recv_sem.at[stage, j],
+            device_id=z_dev(to), device_id_type=MESH,
+        )
+
+    def z_start(stage, j, src, dst):
+        pltpu.make_async_copy(src.at[z], dst.at[z], self_sem.at[stage, j]).start()
+
+        def go(i, _):
+            z_copy(stage, j, src, dst, i).start()
+            return 0
+
+        lax.fori_loop(1, NZ, go, 0)
+
+    def z_wait(stage, j, src, dst):
+        pltpu.make_async_copy(src.at[z], dst.at[z], self_sem.at[stage, j]).wait()
+        pltpu.make_async_copy(src.at[pl.ds(0, NZ - 1)], dst.at[pl.ds(0, NZ - 1)], recv_sem.at[stage, j]).wait()
+
+    def z_sent(stage, j, src, dst):
+        pltpu.make_async_copy(src.at[pl.ds(0, NZ - 1)], dst.at[pl.ds(0, NZ - 1)], send_sem.at[stage, j]).wait()
+
+    def p_start(stage, j, src, dst):
+        def pick(to):
+            if stage == 1:
+                return src.at[to], dst.at[:, :, p]
+            return src.at[:, :, to], dst.at[p]
+
+        a, d = pick(p)
+        pltpu.make_async_copy(a, d, self_sem.at[stage, j]).start()
+
+        def go(i, _):
+            to = lax.rem(p + i, NP)
+            a, d = pick(to)
+            pltpu.make_async_remote_copy(
+                src_ref=a, dst_ref=d, send_sem=send_sem.at[stage, j], recv_sem=recv_sem.at[stage, j],
+                device_id=p_dev(to), device_id_type=MESH,
+            ).start()
+            return 0
+
+        lax.fori_loop(1, NP, go, 0)
+
+    def p_wait(stage, j, flat, whole):
+        a = flat.at[0]
+        pltpu.make_async_copy(a, a, self_sem.at[stage, j]).wait()
+        a = flat.at[pl.ds(0, NP - 1)]
+        pltpu.make_async_copy(a, a, recv_sem.at[stage, j]).wait()
+
+    def p_sent(stage, j, flat):
+        a = flat.at[pl.ds(0, NP - 1)]
+        pltpu.make_async_copy(a, a, send_sem.at[stage, j]).wait()
+
+    def dot(a, bb):
+        return jnp.dot(a, bb, preferred_element_type=jnp.float32)
+
+    def dft(j):
+        w = CHUNKS[j]
+
+        def body(i, _):
+            t = i // 4
+            m = lax.rem(i, 4)
+            rows = fwd[pl.ds(pl.multiple_of(m * 256, 256), 256), :]
+            f = dot(rows, airv[j][t]).astype(jnp.bfloat16)
+            zs1[j][pl.ds(m * 2, 2), t] = f.reshape(2, 128, w)
+            return 0
+
+        lax.fori_loop(0, 8, body, 0)
+
+    def perm1(j):
+        w = CHUNKS[j]
+
+        def body(i, _):
+            part = i // 4
+            g = lax.rem(i, 4)
+            r0 = pl.multiple_of(part * 64 + g * 16, 16)
+            xin = zr1[j][:, :, pl.ds(r0, 16), :].reshape(256, w)
+            yo = dot(q1[...], xin).astype(jnp.bfloat16)
+            ps1[j][pl.ds(g * 8, 8), part] = yo.reshape(8, 2, 16, w)
+            return 0
+
+        lax.fori_loop(0, 8, body, 0)
+
+    def middle(j):
+        w = CHUNKS[j]
+        d0 = offs[j]
+
+        def body(i, _):
+            part = i // 2
+            k = lax.rem(i, 2)
+            xin = mid[j][part, k].reshape(LAT, w)
+            sp = dot(polp[k], xin)
+            sc = (sp * damp[:, d0:d0 + w]).astype(jnp.bfloat16)
+            fo = dot(polt[k], sc).astype(jnp.bfloat16)
+            ret[j][part, k] = fo.reshape(NP, 16, w)
+            return 0
+
+        lax.fori_loop(0, 4, body, 0)
+
+    def perm2(j):
+        w = CHUNKS[j]
+
+        def body(i, _):
+            part = i // 4
+            g = lax.rem(i, 4)
+            r0 = pl.multiple_of(part * 64 + g * 16, 16)
+            xin = pr2[j][pl.ds(g * 8, 8), part].reshape(256, w)
+            yo = dot(q2[...], xin).astype(jnp.bfloat16)
+            zs2[j][:, :, pl.ds(r0, 16), :] = yo.reshape(8, 2, 16, w)
+            return 0
+
+        lax.fori_loop(0, 8, body, 0)
+
+    def inverse(j):
+        w = CHUNKS[j]
+        d0 = offs[j]
+
+        def body(i, _):
+            t = i // 4
+            m = pl.multiple_of(lax.rem(i, 4) * 256, 256)
+            rows = inv[pl.ds(m, 256), :]
+            rec = dot(rows, fin[j][:, t].reshape(N, w)) * (1.0 / 512.0)
+            old = airv[j][t, pl.ds(m, 256), :].astype(jnp.float32)
+            sea = sea_ref[t, pl.ds(m, 256), :]
+            new = old + rec + sea * warm_ref[:, d0:d0 + w]
+            airv[j][t, pl.ds(m, 256), :] = new.astype(jnp.bfloat16)
+            return 0
+
+        lax.fori_loop(0, 8, body, 0)
+        pltpu.make_async_copy(airv[j], out_hbm.at[:, :, pl.ds(d0, w)], out_sem.at[j]).start()
+
+    def prepare():
+        q1[...] = one_hot(256, 256, lambda r, q: (((r & 15) == (q >> 4)) & ((r >> 5) == ((q >> 1) & 7)) & (((r >> 4) & 1) == (q & 1))))
+        q2[...] = one_hot(256, 256, lambda q, r: (((r & 15) == (q >> 4)) & ((r >> 5) == ((q >> 1) & 7)) & (((r >> 4) & 1) == (q & 1))))
+        ld_pol.wait()
+        sel = one_hot(LAT, LAT, lambda r, q: r == true_lat(q))
+        selt = one_hot(LAT, LAT, lambda r, q: true_lat(r) == q)
+        for k in range(2):
+            polp[k] = dot(pol[k], sel).astype(jnp.bfloat16)
+            polt[k] = lax.dot_general(
+                selt, pol[k], (((1,), (1,)), ((), ())), preferred_element_type=jnp.float32
+            ).astype(jnp.bfloat16)
+        ld_damp.wait()
+
+    last = nchunk - 1
+    ld_fwd.wait()
+    ld_air[0].wait()
+    dft(0)
+    pl.semaphore_wait(barrier, NZ - 1 + NP - 1)
+    z_start(0, 0, zs1[0], zr1[0])
+    for j in range(1, nchunk):
+        ld_air[j].wait()
+        dft(j)
+        if j == 1:
+            z_start(0, 1, zs1[1], zr1[1])
+    prepare()
+
+    def step_a(j):
+        z_wait(0, j, zs1[j], zr1[j])
+        if j + 2 <= last:
+            z_start(0, j + 2, zs1[j + 2], zr1[j + 2])
+        perm1(j)
+        p_start(1, j, ps1[j], mid[j])
+
+    def step_b(j):
+        p_wait(1, j, ps1[j], mid[j])
+        middle(j)
+        p_start(2, j, ret[j], pr2[j])
+
+    def step_c(j):
+        p_wait(2, j, pr2[j], pr2[j])
+        perm2(j)
+        z_start(3, j, zs2[j], fin[j])
+
+    def step_d(j):
+        z_wait(3, j, zs2[j], fin[j])
+        if j == 0:
+            ld_inv.wait()
+        inverse(j)
+
+    for i in range(nchunk + 3):
+        if 0 <= i < nchunk:
+            step_a(i)
+        if 0 <= i - 1 < nchunk:
+            step_b(i - 1)
+        if 0 <= i - 2 < nchunk:
+            step_c(i - 2)
+        if 0 <= i - 3 < nchunk:
+            step_d(i - 3)
+
+    for j in range(nchunk):
+        z_sent(0, j, zs1[j], zr1[j])
+        p_sent(1, j, ps1[j])
+        p_sent(2, j, pr2[j])
+        z_sent(3, j, zs2[j], fin[j])
+        pltpu.make_async_copy(airv[j], out_hbm.at[:, :, pl.ds(offs[j], CHUNKS[j])], out_sem.at[j]).wait()
+
+
+def spectral(air, fwd, inv, pol, damp, warm, sea):
+    bf = jnp.bfloat16
+    n = len(CHUNKS)
+    scratch = [
+        pltpu.VMEM((N, N), bf), pltpu.VMEM((N, N), bf),
+        pltpu.VMEM((2, LAT, LAT), bf), pltpu.VMEM((2, LAT, LAT), bf), pltpu.VMEM((2, LAT, LAT), bf),
+        pltpu.VMEM((LAT, 768), jnp.float32), pltpu.VMEM((256, 256), bf), pltpu.VMEM((256, 256), bf),
+    ]
+    scratch += [pltpu.VMEM((2, N, w), bf) for w in CHUNKS]
+    scratch += [pltpu.VMEM((NZ, 2, 128, w), bf) for w in CHUNKS]
+    scratch += [pltpu.VMEM((NZ, 2, 128, w), bf) for w in CHUNKS]
+    scratch += [pltpu.VMEM((NP, 2, 2, 16, w), bf) for w in CHUNKS]
+    scratch += [pltpu.VMEM((2, 2, NP, 16, w), bf) for w in CHUNKS]
+    scratch += [pltpu.VMEM((2, 2, NP, 16, w), bf) for w in CHUNKS]
+    scratch += [pltpu.VMEM((NP, 2, 2, 16, w), bf) for w in CHUNKS]
+    scratch += [pltpu.VMEM((NZ, 2, 128, w), bf) for w in CHUNKS]
+    scratch += [pltpu.VMEM((NZ, 2, 128, w), bf) for w in CHUNKS]
+    dma = pltpu.SemaphoreType.DMA
+    scratch += [dma((4 + n,)), dma((n,)), dma((4, n)), dma((4, n)), dma((4, n))]
+    anys = pl.BlockSpec(memory_space=pl.ANY)
+    vm = pl.BlockSpec(memory_space=pltpu.VMEM)
+    return pl.pallas_call(
+        spectral_kernel,
+        out_shape=jax.ShapeDtypeStruct(air.shape, bf),
+        in_specs=[anys] * 5 + [vm] * 2,
+        out_specs=anys,
+        scratch_shapes=scratch,
+        compiler_params=pltpu.CompilerParams(
+            collective_id=0, has_side_effects=True, vmem_limit_bytes=60 << 20
+        ),
+        name="spectral",
+    )(air, fwd, inv, pol, damp, warm, sea)
 
 
 def ocean_update(
@@ -86,9 +423,6 @@
     sec_count = lax.axis_size("sec")
     band_count = lax.axis_size("band")
     core_count = lax.axis_size("ch")
-    device_count = sec_count * band_count * core_count
-    total_cols = 2 * K
-    per_device = total_cols // device_count
     slot_count = water_patch_fields.shape[0]
     flux_local = jnp.einsum(
         "anc,cf->fan",
@@ -142,52 +476,17 @@
         "jk,krw->rjw", selector, sea_all, preferred_element_type=jnp.float32
     ).astype(jnp.bfloat16)
     water_skin_warmth = water_patches.reshape(parallel_lines, meridian_number)
-    mode_count = associated_polynomial_matrix.shape[0]
-    lat_count = associated_polynomial_matrix.shape[1]
-    sb_count = sec_count * band_count
-    column_order = jnp.arange(total_cols, dtype=jnp.int32)
-    forward, inverse = dft_tables(meridian_number, column_order)
-    fourier = jnp.einsum(
-        "nq,anc->qac", forward, air_field_lattice, preferred_element_type=jnp.float32
-    ).astype(jnp.bfloat16)
-    collected = lax.all_to_all(
-        lax.all_to_all(fourier, ("sec", "band"), split_axis=0, concat_axis=1, tiled=True),
-        "ch",
-        split_axis=0,
-        concat_axis=1,
-        tiled=True,
-    )
-    transform_local = associated_polynomial_matrix.reshape(
-        mode_count, lat_count, sb_count, core_count, parallel_lines
-    )
-    transform_local = transform_local.transpose(0, 1, 3, 2, 4).reshape(
-        mode_count, lat_count, lat_count
-    )
-    coeff_pairs = collected.reshape(mode_count, 2, lat_count, channel_count)
-    spectrum = jnp.einsum(
-        "mlt,mptc->mplc", transform_local, coeff_pairs, preferred_element_type=jnp.float32
-    )
-    scaled = (spectrum * harmonic_damping_factor[None, None]).astype(jnp.bfloat16)
-    damped_modes = jnp.einsum(
-        "mlt,mplc->mptc", transform_local, scaled, preferred_element_type=jnp.float32
-    )
-    damped_modes = damped_modes.astype(jnp.bfloat16).reshape(per_device, lat_count, channel_count)
-    returned = lax.all_to_all(
-        lax.all_to_all(damped_modes, "ch", split_axis=1, concat_axis=0, tiled=True),
-        ("sec", "band"),
-        split_axis=1,
-        concat_axis=0,
-        tiled=True,
-    )
-    reconstruct_physical = jnp.einsum(
-        "qn,qac->anc", inverse, returned, preferred_element_type=jnp.float32
-    )
-    advanced_pair = (
-        air_field_lattice.astype(jnp.float32)
-        + reconstruct_physical
-        + water_skin_warmth.astype(jnp.float32)[:, :, None] * warmth_response_factor[None, None, :]
-    )
-    return (advanced_pair.astype(jnp.bfloat16), ocean_next)
+    fwd, inv = basis_tables()
+    advanced = spectral(
+        air_field_lattice,
+        fwd,
+        inv,
+        associated_polynomial_matrix,
+        harmonic_damping_factor,
+        warmth_response_factor[None, :],
+        water_skin_warmth.astype(jnp.float32)[:, :, None],
+    )
+    return (advanced, ocean_next)
 
 
 def solution(mesh):

time: 389 us -> 393 us (1.010)
  the two profiles are of different devices: /device:TPU:32 before, /device:TPU:1 now
where the time goes in v1:
time: 393 us
  Pallas kernels  179 us (46%)
  blocking collectives  94.2 us (24%)
  waiting for transfers between devices  56.5 us (14%)
  matrix products  25.1 us (6%)
  local copies, waits for them, and re-layouts  18.5 us (5%)
  between operations  14.3 us (4%)
  other arithmetic  5.31 us (1%)
    pallas_call x1, Pallas kernels, spectral(): pl.pallas_call(spectral_kernel, out_shape=jax.ShapeDtypeStruct(air.shape,...  179 us
    all_gather x1, blocking collectives, shards(): sea_all = lax.all_gather(sea_slots, 'band', axis=0, tiled=True)  94.2 us
    all_gather x1, waiting for transfers between devices, shards(): gathered = lax.all_gather(flux_local, 'band', axis=1, tiled=True)  56.5 us
    dot_general x9, matrix products, ocean_update(): jnp.einsum('io,sirw->sorw', kernel_coefficients[shift_row, shift_col], wi...  13.9 us
  transfers between devices with their start and end apart: 1, of which 1 were waited for; matrix products, arithmetic and copies ran while one was open for 7% of the time, Pallas kernels for 0%

profile of v1, /device:TPU:1, one launch (start us, length us, event | category | flops | bytes accessed | tf_op | source)
XLA Modules:
  0.0 392.9 jit_solution(9891585791131108871)
XLA Ops:
  7.3 3.6 convolution_convert_fusion
  11.7 7.5 %fusion.77 = (bf16[6,128,2,256]{1,2,3,0:T(2,128)(2,1)S(1)}, bf16[6,128,2,256]{1,2,3,0:T(2,128)(2,1)S(1)}, bf16[6,128,2,256]{1,2,3,0:T(2,128)(2,1)S(1)}, bf16[6,1...) fusion(bf16[6,128,4,258]{1,2,3,0:T(4,128)(2,1)S(1)} %copy-done.1), kind=kLoop, calls=%fused_computation.94 | loop fusion | bytes 14155776 | tf_op jit(solution)/shard_map/slice | solution.py:385
  19.2 1.6 fusion.37
  20.7 1.5 fusion.15
  22.3 1.5 fusion.17
  23.8 1.5 fusion.19
  25.3 0.8 fusion.72
  26.4 0.6 broadcast_in_dim.5.warm_ref
  27.0 1.6 fusion.21
  28.6 1.5 fusion.23
  30.1 1.6 fusion.25
  31.7 1.5 fusion.27
  33.3 1.5 fusion.29
  34.9 2.0 add_convert_fusion
  36.9 2.1 add_convert_fusion.1
  38.9 56.5 %all-gather.3.cloned.1.call-done = bf16[8,64,1024]{2,0,1:T(8,128)(2,1)} async-done(((bf16[8,2,1024]{2,0,1:T(8,128)(2,1)}), bf16[8,64,1024]{2,0,1:T(8,128)(2,1)}) %all-gather.3.cloned.1.call-update) | async-done | bytes 1048592 | tf_op jit(solution)/shard_map/all_gather | solution.py:433
  95.5 1.9 reshape.128
  97.3 0.8 convert_reduce_fusion
  98.3 6.7 %fusion.9 = bf16[6,128,2,256]{1,3,2,0:T(8,128)(2,1)S(1)} fusion(f32[6,2,256,128]{3,2,1,0:T(8,128)} %fusion.15, f32[6,2,256,128]{3,2,1,0:T(8,128)} %fusion.17, f32[6,2,256,128]{3,2,1,0:T(8,128)} %fusion.19, f32[6,2,256,128]{3,2,1,0:T(8,128)} %fusion.21, f32[6,2,256,128]{3,2,1,0:T(8,128)} %fusion.37, f32[6,2,256,128]{3,2,1,0:T(8,128)} %fusion.23, ...), kind=kOutput, calls=%fused_computation.13 | convolution fusion | flops 116391936 | bytes 15828480 | tf_op jit(solution)/shard_map/io,sirw->sorw/dot_general | solution.py:397
  105.0 1.8 copy.129
  107.1 94.2 %all-gather = bf16[192,1,2,256]{3,2,1,0:T(2,128)(2,1)S(1)} all-gather(bf16[6,1,2,256]{3,2,1,0:T(2,128)(2,1)S(1)} %copy.126), channel_id=2, replica_groups=mesh['sec'=4,'band'=32,'ch'=2] {'band'}, dimensions={0}, use_global_device_ids=true | all-gather | bytes 202752 | tf_op jit(solution)/shard_map/all_gather | solution.py:467
  201.5 1.9 reshape.129.sea_ref
  203.4 178.9 %spectral.1 = bf16[2,1024,768]{2,1,0:T(8,128)(2,1)} custom-call(bf16[2,1024,768]{2,1,0:T(8,128)(2,1)} %air_hbm.1, bf16[1024,1024]{1,0:T(8,128)(2,1)} %bitcast.114, bf16[1024,1024]{1,0:T(8,128)(2,1)} %bitcast.113, bf16[2,512,512]{2,1,0:T(8,128)(2,1)} %pol_hbm.1, f32[512,768]{1,0:T(8,128)} %damp_hbm.1, f32[1,768]{1,0:T(1,128)} %broadcast_in_dim.5.warm_ref, ...), custom_call_target="tpu_custom_call" | custom-call | tf_op jit(solution)/shard_map/spectral/pallas_call | solution.py:348
  382.3 3.8 copy.190
  (67 shorter events, 1.8 us)
Async XLA Ops:
  7.2 91.1 %copy-start = (bf16[128,128]{1,0:T(8,128)(2,1)S(1)}, bf16[128,128]{1,0:T(8,128)(2,1)}, u32[]{:S(2)}) copy-start(bf16[128,128]{1,0:T(8,128)(2,1)} %param.32) | copy-start | bytes 98308
  7.2 3.7 copy-start.17
  7.2 4.4 %copy-start.16 = (s32[6,2,256]{2,1,0:T(2,128)S(1)}, s32[6,2,256]{2,1,0:T(2,128)}, u32[]{:S(2)}) copy-start(s32[6,2,256]{2,1,0:T(2,128)} %param.34) | copy-start | bytes 36868
  7.2 4.5 %copy-start.22 = (s32[6]{0:T(128)S(1)}, s32[6]{0:T(128)}, u32[]{:S(2)}) copy-start(s32[6]{0:T(128)} %param.35) | copy-start | bytes 76
  7.2 4.5 %copy-start.1 = (bf16[6,128,4,258]{1,2,3,0:T(4,128)(2,1)S(1)}, bf16[6,128,4,258]{1,2,3,0:T(4,128)(2,1)}, u32[]{:S(2)}) copy-start(bf16[6,128,4,258]{1,2,3,0:T(4,128)(2,1)} %param.27) | copy-start | bytes 4755460
  7.2 88.2 %all-gather.3.cloned.1.call-start = ((), (), s32[]{:S(2)}) async-start(), calls=%async_computation | async-start | bytes 1081344 | tf_op jit(solution)/shard_map/all_gather | solution.py:433
  11.0 0.7 copy-start.9
  11.7 7.5 %copy-start.6 = (bf16[3,3,128,128]{3,2,1,0:T(8,128)(2,1)S(1)}, bf16[3,3,128,128]{3,2,1,0:T(8,128)(2,1)}, u32[]{:S(2)}) copy-start(bf16[3,3,128,128]{3,2,1,0:T(8,128)(2,1)} %param.28) | copy-start | bytes 884740
  23.8 2.6 copy-start.19
  23.8 3.2 copy-start.5
  25.3 3.3 copy-start.4
  28.6 1.5 copy-start.3
  30.1 1.6 copy-start.2
  33.2 1.5 copy-start.10
  33.3 1.5 copy-start.11
  33.3 1.5 copy-start.12
  33.3 1.5 copy-start.13
  34.8 2.1 copy-start.7
  34.8 2.0 copy-start.8
  34.8 2.0 copy-start.14
  34.8 2.0 copy-start.15
  38.9 59.3 %copy-start.18 = (f32[8,128]{1,0:T(8,128)S(1)}, f32[8,128]{1,0:T(8,128)}, u32[]{:S(2)}) copy-start(f32[8,128]{1,0:T(8,128)} %param.30) | copy-start | bytes 12292
  38.9 59.4 %copy-start.20 = (bf16[8,128]{1,0:T(8,128)(2,1)S(1)}, bf16[8,128]{1,0:T(8,128)(2,1)}, u32[]{:S(2)}) copy-start(bf16[8,128]{1,0:T(8,128)(2,1)} %param.29) | copy-start | bytes 6148
  38.9 59.4 %copy-start.21 = (f32[128]{0:T(128)S(1)}, f32[128]{0:T(128)}, u32[]{:S(2)}) copy-start(f32[128]{0:T(128)} %param.31) | copy-start | bytes 1540
Sparse Core Ops, SparseCore 0:
  11.5 83.9 all-gather.2

commit v2 on v1

--- a/solution.py
+++ b/solution.py
@@ -63,7 +63,9 @@
 
 
 def spectral_kernel(
-    air_hbm, fwd_hbm, inv_hbm, pol_hbm, damp_hbm, warm_ref, sea_ref, out_hbm, *scr
+    air_hbm, fwd_hbm, inv_hbm, pol_hbm, damp_hbm, patch_hbm, warm_ref, proj_ref, conv_ref,
+    local_ref, mean_ref, bias_ref, read_ref, wet_ref, total_ref, slot_ref, owner_ref, rank_ref,
+    out_hbm, ocean_hbm, *scr
 ):
     nchunk = len(CHUNKS)
     it = iter(scr)
@@ -77,7 +79,8 @@
     pr2 = [next(it) for _ in CHUNKS]
     zs2 = [next(it) for _ in CHUNKS]
     fin = [next(it) for _ in CHUNKS]
-    load_sem, out_sem, send_sem, recv_sem, self_sem = (next(it) for _ in range(5))
+    patch, x3, q3, q4, fpair, fall, spair, sall, seab, ocean = (next(it) for _ in range(10))
+    load_sem, out_sem, send_sem, recv_sem, self_sem, xs_sem = (next(it) for _ in range(6))
 
     s = lax.axis_index("sec")
     b = lax.axis_index("band")
@@ -87,6 +90,7 @@
     x = lax.rem(b, 4)
     z = z_hi * 4 + s
     p = y * 8 + x * 2 + c
+    yx = y * 4 + x
 
     def z_dev(zz):
         return (lax.rem(zz, 4), y * 8 + (zz // 4) * 4 + x, c)
@@ -111,6 +115,7 @@
     ld_pol = load(pol_hbm, pol)
     ld_damp = load(damp_hbm, damp)
     ld_inv = load(inv_hbm, inv)
+    ld_patch = load(patch_hbm, patch)
 
     barrier = pltpu.get_barrier_semaphore()
 
@@ -181,6 +186,104 @@
 
     def dot(a, bb):
         return jnp.dot(a, bb, preferred_element_type=jnp.float32)
+
+    def flip_copy(stage, buf):
+        return pltpu.make_async_remote_copy(
+            src_ref=buf.at[z_hi], dst_ref=buf.at[z_hi], send_sem=xs_sem.at[stage, 0], recv_sem=xs_sem.at[stage, 1],
+            device_id=z_dev(lax.rem(z + 4, NZ)), device_id_type=MESH,
+        )
+
+    def spread_start(stage, pair, whole):
+        pltpu.make_async_copy(pair, whole.at[yx], xs_sem.at[stage, 2]).start()
+
+        def go(i, _):
+            to = lax.rem(yx + i, 16)
+            pltpu.make_async_remote_copy(
+                src_ref=pair, dst_ref=whole.at[yx], send_sem=xs_sem.at[stage, 3], recv_sem=xs_sem.at[stage, 4],
+                device_id=p_dev(to * 2 + c), device_id_type=MESH,
+            ).start()
+            return 0
+
+        lax.fori_loop(1, 16, go, 0)
+
+    def spread_wait(stage, pair, whole):
+        pltpu.make_async_copy(pair, whole.at[yx], xs_sem.at[stage, 2]).wait()
+        a = whole.at[pl.ds(0, 15)]
+        pltpu.make_async_copy(a, a, xs_sem.at[stage, 4]).wait()
+
+    def spread_sent(stage, whole):
+        a = whole.at[pl.ds(0, 15)]
+        pltpu.make_async_copy(a, a, xs_sem.at[stage, 3]).wait()
+
+    def dot_t(a, bb):
+        return lax.dot_general(a, bb, (((1,), (1,)), ((), ())), preferred_element_type=jnp.float32)
+
+    def surface_flux():
+        for j in range(nchunk):
+            ld_air[j].wait() if j else None
+        for t in range(2):
+            acc = None
+            for j in range(nchunk):
+                part = dot_t(proj_ref[:, offs[j]:offs[j] + CHUNKS[j]], airv[j][t])
+                acc = part if acc is None else acc + part
+            acc = acc.astype(jnp.bfloat16)
+            for q in range(4):
+                fpair[z_hi, q, t] = acc[:, q * 256:(q + 1) * 256]
+
+    def rows_first(i, _):
+        for blk in range(4):
+            rows = patch[i, blk * 256:(blk + 1) * 256, :]
+            x3[i, :, blk * 64:(blk + 1) * 64, :] = dot(q3[...], rows).reshape(4, 64, 128)
+        x3[i, :, 256:264, :] = dot(q4[...], patch[i, 776:1032, :]).reshape(4, 8, 128)
+        return 0
+
+    def ocean_step(i, sea):
+        tile = slot_ref[i]
+        owner_b = tile >> 2
+        flux = fall[((owner_b >> 3) << 2) + (owner_b & 3), (owner_b >> 2) & 1, tile & 3].astype(jnp.float32)
+        wet = wet_ref[i].astype(jnp.float32)
+        masked = [flux[r] * wet[r:r + 1, :] for r in range(2)]
+        whole = jnp.sum(masked[0] + masked[1], axis=1, keepdims=True)
+        fmean = whole / jnp.maximum(total_ref[i].astype(jnp.float32), 1.0)
+        shift = bias_ref[...]
+        for f in range(8):
+            shift = shift + mean_ref[:, f:f + 1] * fmean[f:f + 1, :]
+        for r in range(2):
+            wins = [
+                x3[i, r + dr, dw:dw + 256, :].astype(jnp.bfloat16) for dr in range(3) for dw in range(3)
+            ]
+            pre = dot_t(conv_ref[...], jnp.concatenate(wins, axis=1))
+            pre = pre + dot(local_ref[...], masked[r].astype(jnp.bfloat16)) + shift
+            hidden = jax.nn.gelu(pre, approximate=True).astype(jnp.bfloat16)
+            old = dot_t(read_ref[1], wins[4])
+            new = (old + dot(read_ref[0], hidden)) * wet[r:r + 1, :]
+            ocean[i, r] = new.astype(jnp.bfloat16)
+            line = lax.broadcasted_iota(jnp.int32, (16, 256), 0)
+            sea = jnp.where(line == 2 * i + r, jnp.broadcast_to(new[0:1, :], (16, 256)), sea)
+        return sea
+
+    def ocean_all():
+        q3[...] = one_hot(256, 256, lambda r, q: ((r >> 6) == (q & 3)) & ((r & 63) == (q >> 2)))
+        q4[...] = one_hot(32, 256, lambda r, q: q == (r & 7) * 4 + (r >> 3) + 248)
+        ld_patch.wait()
+        lax.fori_loop(0, 6, rows_first, 0)
+        spread_wait(0, fpair, fall)
+        sea = lax.fori_loop(0, 6, ocean_step, jnp.zeros((16, 256), jnp.float32))
+        spair[z_hi] = sea.astype(jnp.bfloat16)
+        flip_copy(1, spair).start()
+        pltpu.make_async_copy(ocean, ocean_hbm, xs_sem.at[0, 5]).start()
+
+    def place_sea():
+        spread_wait(1, spair, sall)
+        for q in range(4):
+            at = (lax.axis_index("band")) * 4 + q
+            owner = owner_ref[at]
+            slot = rank_ref[at]
+            tile = sall[((owner >> 3) << 2) + (owner & 3), (owner >> 2) & 1].astype(jnp.float32)
+            for t in range(2):
+                line = lax.broadcasted_iota(jnp.int32, (16, 256), 0)
+                row = jnp.sum(jnp.where(line == 2 * slot + t, tile, 0.0), axis=0, keepdims=True)
+                seab[t, q * 256:(q + 1) * 256, :] = jnp.broadcast_to(row, (128, 256)).T
 
     def dft(j):
         w = CHUNKS[j]
@@ -249,7 +352,8 @@
             rows = inv[pl.ds(m, 256), :]
             rec = dot(rows, fin[j][:, t].reshape(N, w)) * (1.0 / 512.0)
             old = airv[j][t, pl.ds(m, 256), :].astype(jnp.float32)
-            sea = sea_ref[t, pl.ds(m, 256), :]
+            sea = seab[t, pl.ds(m, 256), :]
+            sea = jnp.concatenate([sea] * (w // 128), axis=1)
             new = old + rec + sea * warm_ref[:, d0:d0 + w]
             airv[j][t, pl.ds(m, 256), :] = new.astype(jnp.bfloat16)
             return 0
@@ -276,12 +380,15 @@
     dft(0)
     pl.semaphore_wait(barrier, NZ - 1 + NP - 1)
     z_start(0, 0, zs1[0], zr1[0])
+    surface_flux()
+    flip_copy(0, fpair).start()
     for j in range(1, nchunk):
-        ld_air[j].wait()
         dft(j)
         if j == 1:
             z_start(0, 1, zs1[1], zr1[1])
     prepare()
+    flip_copy(0, fpair).wait()
+    spread_start(0, fpair, fall)
 
     def step_a(j):
         z_wait(0, j, zs1[j], zr1[j])
@@ -309,6 +416,13 @@
     for i in range(nchunk + 3):
         if 0 <= i < nchunk:
             step_a(i)
+        if i == 0:
+            ocean_all()
+        if i == 1:
+            flip_copy(1, spair).wait()
+            spread_start(1, spair, sall)
+        if i == 3:
+            place_sea()
         if 0 <= i - 1 < nchunk:
             step_b(i - 1)
         if 0 <= i - 2 < nchunk:
@@ -316,6 +430,9 @@
         if 0 <= i - 3 < nchunk:
             step_d(i - 3)
 
+    spread_sent(0, fall)
+    spread_sent(1, sall)
+    pltpu.make_async_copy(ocean, ocean_hbm, xs_sem.at[0, 5]).wait()
     for j in range(nchunk):
         z_sent(0, j, zs1[j], zr1[j])
         p_sent(1, j, ps1[j])
@@ -324,7 +441,7 @@
         pltpu.make_async_copy(airv[j], out_hbm.at[:, :, pl.ds(offs[j], CHUNKS[j])], out_sem.at[j]).wait()
 
 
-def spectral(air, fwd, inv, pol, damp, warm, sea):
+def spectral(air, fwd, inv, pol, damp, patch, *rest):
     bf = jnp.bfloat16
     n = len(CHUNKS)
     scratch = [
@@ -341,66 +458,29 @@
     scratch += [pltpu.VMEM((NP, 2, 2, 16, w), bf) for w in CHUNKS]
     scratch += [pltpu.VMEM((NZ, 2, 128, w), bf) for w in CHUNKS]
     scratch += [pltpu.VMEM((NZ, 2, 128, w), bf) for w in CHUNKS]
+    scratch += [
+        pltpu.VMEM((6, 1032, 128), bf), pltpu.VMEM((6, 4, 264, 128), jnp.float32),
+        pltpu.VMEM((256, 256), bf), pltpu.VMEM((32, 256), bf),
+        pltpu.VMEM((2, 4, 2, 8, 256), bf), pltpu.VMEM((16, 2, 4, 2, 8, 256), bf),
+        pltpu.VMEM((2, 16, 256), bf), pltpu.VMEM((16, 2, 16, 256), bf),
+        pltpu.VMEM((2, N, 128), jnp.float32), pltpu.VMEM((6, 2, 128, 256), bf),
+    ]
     dma = pltpu.SemaphoreType.DMA
-    scratch += [dma((4 + n,)), dma((n,)), dma((4, n)), dma((4, n)), dma((4, n))]
+    scratch += [dma((5 + n,)), dma((n,)), dma((4, n)), dma((4, n)), dma((4, n)), dma((2, 6))]
     anys = pl.BlockSpec(memory_space=pl.ANY)
     vm = pl.BlockSpec(memory_space=pltpu.VMEM)
+    sm = pl.BlockSpec(memory_space=pltpu.SMEM)
     return pl.pallas_call(
         spectral_kernel,
-        out_shape=jax.ShapeDtypeStruct(air.shape, bf),
-        in_specs=[anys] * 5 + [vm] * 2,
-        out_specs=anys,
+        out_shape=(jax.ShapeDtypeStruct(air.shape, bf), jax.ShapeDtypeStruct((6, 2, 128, 256), bf)),
+        in_specs=[anys] * 6 + [vm] * 8 + [sm] * 4,
+        out_specs=(anys, anys),
         scratch_shapes=scratch,
         compiler_params=pltpu.CompilerParams(
             collective_id=0, has_side_effects=True, vmem_limit_bytes=60 << 20
         ),
         name="spectral",
-    )(air, fwd, inv, pol, damp, warm, sea)
-
-
-def ocean_update(
-    state,
-    tile_flux,
-    mask_tile,
-    count_tile,
-    kernel_coefficients,
-    local_exchange_matrix,
-    patch_average_matrix,
-    water_kernel_offset,
-    water_readout_matrix,
-):
-    parallel_lines = mask_tile.shape[1]
-    tile_width = mask_tile.shape[2]
-    mask_f = mask_tile.astype(jnp.float32)
-    masked = tile_flux * mask_tile[:, None].astype(jnp.bfloat16)
-    fmean = (
-        jnp.sum(masked.astype(jnp.float32), axis=(2, 3))
-        / jnp.maximum(count_tile.astype(jnp.float32), 1.0)[:, None]
-    )
-    total = jnp.einsum(
-        "fo,sfrw->sorw", local_exchange_matrix, masked, preferred_element_type=jnp.float32
-    )
-    for shift_row in range(3):
-        for shift_col in range(3):
-            window = state[
-                :, :, shift_row : shift_row + parallel_lines, shift_col : shift_col + tile_width
-            ]
-            total = total + jnp.einsum(
-                "io,sirw->sorw",
-                kernel_coefficients[shift_row, shift_col],
-                window,
-                preferred_element_type=jnp.float32,
-            )
-    mean_term = jnp.sum(fmean[:, :, None] * patch_average_matrix[None], axis=1)
-    total = total + mean_term[:, :, None, None] + water_kernel_offset[None, :, None, None]
-    hidden = jax.nn.gelu(total, approximate=True).astype(jnp.bfloat16)
-    update = jnp.einsum(
-        "io,sirw->sorw", water_readout_matrix, hidden, preferred_element_type=jnp.float32
-    )
-    fresh = (
-        state[:, :, 1 : 1 + parallel_lines, 1 : 1 + tile_width].astype(jnp.float32) + update
-    ) * mask_f[:, None]
-    return fresh.astype(jnp.bfloat16)
+    )(air, fwd, inv, pol, damp, patch, *rest)
 
 
 def shards(
@@ -419,74 +499,43 @@
     water_point_indicator,
     water_point_totals,
 ):
-    parallel_lines, meridian_number, channel_count = air_field_lattice.shape
-    sec_count = lax.axis_size("sec")
-    band_count = lax.axis_size("band")
-    core_count = lax.axis_size("ch")
-    slot_count = water_patch_fields.shape[0]
-    flux_local = jnp.einsum(
-        "anc,cf->fan",
-        air_field_lattice,
-        boundary_exchange_projector,
-        preferred_element_type=jnp.float32,
-    ).astype(jnp.bfloat16)
-    gathered = lax.all_gather(flux_local, "band", axis=1, tiled=True)
     sec_id = lax.axis_index("sec")
     band_id = lax.axis_index("band")
     core_id = lax.axis_index("ch")
-    owner_grid = patch_holder_index.reshape(sec_count, band_count, core_count, -1)
-    tiles_per_row = owner_grid.shape[3]
-    owner_group = lax.dynamic_index_in_dim(owner_grid, sec_id, 0, keepdims=False)
-    owner_group = lax.dynamic_index_in_dim(owner_group, core_id, 1, keepdims=False)
-    owner_flat = owner_group.reshape(-1)
-    holders = jnp.arange(band_count, dtype=jnp.int32)
-    mine_all = owner_flat[None, :] == holders[:, None]
-    rank_all = jnp.cumsum(mine_all.astype(jnp.int32), axis=1) - 1
-    slot_index = jnp.arange(slot_count, dtype=jnp.int32)
-    pick_all = mine_all[:, None, :] & (rank_all[:, None, :] == slot_index[None, :, None])
-    my_pick = lax.dynamic_index_in_dim(pick_all, band_id, 0, keepdims=False)
-    flux_count = gathered.shape[0]
-    tile_width = meridian_number // tiles_per_row
-    pieces = gathered.reshape(flux_count, band_count, parallel_lines, tiles_per_row, tile_width)
-    chooser = my_pick.reshape(slot_count, band_count, tiles_per_row).astype(jnp.bfloat16)
-    tile_flux = jnp.einsum(
-        "sbj,fbrjw->sfrw", chooser, pieces, preferred_element_type=jnp.float32
-    ).astype(jnp.bfloat16)
-    ocean_next = ocean_update(
-        water_patch_fields,
-        tile_flux,
-        water_point_indicator,
-        water_point_totals,
-        kernel_coefficients,
-        local_exchange_matrix,
-        patch_average_matrix,
-        water_kernel_offset,
-        water_readout_matrix,
-    )
-    sea_slots = ocean_next[:, 0]
-    sea_all = lax.all_gather(sea_slots, "band", axis=0, tiled=True)
-    rank_tile = jnp.sum(jnp.where(mine_all, rank_all, 0), axis=0)
-    my_owners = lax.dynamic_index_in_dim(owner_group, band_id, 0, keepdims=False)
-    my_ranks = lax.dynamic_slice_in_dim(rank_tile, band_id * tiles_per_row, tiles_per_row)
-    target = my_owners * slot_count + my_ranks
-    selector = (
-        target[:, None] == jnp.arange(band_count * slot_count, dtype=jnp.int32)[None, :]
-    ).astype(jnp.bfloat16)
-    water_patches = jnp.einsum(
-        "jk,krw->rjw", selector, sea_all, preferred_element_type=jnp.float32
-    ).astype(jnp.bfloat16)
-    water_skin_warmth = water_patches.reshape(parallel_lines, meridian_number)
+    owner_grid = patch_holder_index.reshape(4, 32, 2, 4)
+    owners = lax.dynamic_slice(owner_grid, (sec_id, 0, core_id, 0), (1, 32, 1, 4)).reshape(128)
+    at = jnp.arange(128, dtype=jnp.int32)
+    same = owners[:, None] == owners[None, :]
+    ranks = jnp.sum((same & (at[None, :] < at[:, None])).astype(jnp.int32), axis=1)
+    slot = jnp.arange(6, dtype=jnp.int32)
+    chosen = (owners[None, :] == band_id) & (ranks[None, :] == slot[:, None])
+    slot_tile = jnp.sum(jnp.where(chosen, at[None, :], 0), axis=1)
     fwd, inv = basis_tables()
-    advanced = spectral(
+    bf = jnp.bfloat16
+    conv = kernel_coefficients.reshape(9 * 128, 128).T
+    readout = jnp.stack([water_readout_matrix.T, jnp.eye(128, dtype=bf)])
+    patches = water_patch_fields.transpose(0, 3, 2, 1).reshape(6, 1032, 128)
+    advanced, ocean = spectral(
         air_field_lattice,
         fwd,
         inv,
         associated_polynomial_matrix,
         harmonic_damping_factor,
+        patches,
         warmth_response_factor[None, :],
-        water_skin_warmth.astype(jnp.float32)[:, :, None],
+        boundary_exchange_projector.T,
+        conv,
+        local_exchange_matrix.T,
+        patch_average_matrix.T,
+        water_kernel_offset[:, None],
+        readout,
+        water_point_indicator,
+        water_point_totals,
+        slot_tile,
+        owners,
+        ranks,
     )
-    return (advanced, ocean_next)
+    return (advanced, ocean.transpose(0, 2, 1, 3))
 
 
 def solution(mesh):

time: 393 us -> 207 us (0.53); the launches traced: 393 us -> 203 us
  blocking collectives: 94.2 us -> 0 us
  waiting for transfers between devices: 56.5 us -> 0 us
  matrix products: 25.1 us -> 0 us
  between operations: 14.3 us -> 0.75 us
    all_gather x1 -> x0, blocking collectives: 94.2 us -> none  [shards(): sea_all = lax.all_gather(sea_slots, 'band', axis=0, tiled=True)]
    all_gather x1 -> x0, waiting for transfers between devices: 56.5 us -> none  [shards(): gathered = lax.all_gather(flux_local, 'band', axis=1, tiled=True)]
    dot_general x13 -> x0, matrix products: 25.1 us -> none  [the longest x9 13.9 us: ocean_update(): jnp.einsum('io,sirw->sorw', kernel_coefficients[shift_row, shift_col], wi...]
    slice x2 -> x0, local copies, waits for them, and re-layouts: 7.77 us -> none  [the longest x1 7.46 us: ocean_update(): state[:, :, shift_row:shift_row + parallel_lines, shift_col:shift_col + t...]
    unnamed x49 -> x18, local copies, waits for them, and re-layouts: 5.88 us -> 11.1 us
  transfers between devices with their start and end apart: 1 -> 0, of which waited for: 1 -> 0; matrix products, arithmetic and copies ran while one was open for 7% -> 0% of each run, Pallas kernels for 0% -> 0%
where the time goes in v2:
time: 207 us; the launch traced here: 203 us
  Pallas kernels  180 us (87%)
  local copies, waits for them, and re-layouts  15.8 us (8%)
  other arithmetic  6.64 us (3%)
    pallas_call x1, Pallas kernels, spectral(): pl.pallas_call(spectral_kernel, out_shape=(jax.ShapeDtypeStruct(air.shape...  180 us
    unnamed x18, local copies, waits for them, and re-layouts  11.1 us

profile of v2, /device:TPU:1, one launch (start us, length us, event | category | flops | bytes accessed | tf_op | source)
XLA Modules:
  0.0 202.7 jit_solution(12324415086254045533)
XLA Ops:
  0.6 0.0 copy-start
  0.6 0.0 copy-start.1
  0.7 0.0 copy-start.2
  0.7 0.0 copy-start.3
  0.7 1.4 broadcast_in_dim.16.warm_ref
  2.0 1.4 copy.39
  3.4 0.9 copy.41
  4.3 0.6 pad_maximum_fusion.read_ref
  4.9 1.4 copy.40
  6.3 1.4 copy.43.bias_ref
  7.7 0.8 copy.42
  8.5 0.1 dynamic-slice_reduce_fusion
  8.6 0.1 broadcast_in_dim_reshape.2.owner_ref
  8.7 0.0 copy-start.4
  8.7 0.2 convert_reduce_fusion.rank_ref
  8.9 0.0 copy-start.5
  8.9 0.7 select_reduce_fusion.slot_ref
  9.6 1.8 copy.38
  11.5 3.1 %add_convert_fusion.1 = bf16[64,16,1024]{2,1,0:T(8,128)(2,1)} fusion(f32[16,1024]{1,0:T(8,128)} %constant.39.clone, f32[64,1024]{1,0:T(8,128)} %constant.38.clone, f32[16,1024]{1,0:T(8,128)} %constant.37.clone, f32[64,1024]{1,0:T(8,128)} %constant.36.clone), kind=kLoop, calls=%fused_computation.1 | loop fusion | flops 4194304 | bytes 2752512 | tf_op jit(solution)/shard_map/convert_element_type | solution.py:37
  14.6 0.0 copy-done.1
  14.6 2.0 add_convert_fusion
  16.6 179.5 %spectral.1 = (bf16[2,1024,768]{2,1,0:T(8,128)(2,1)}, bf16[6,2,128,256]{3,2,1,0:T(8,128)(2,1)}) custom-call(bf16[2,1024,768]{2,1,0:T(8,128)(2,1)} %air_hbm.1, bf16[1024,1024]{1,0:T(8,128)(2,1)} %bitcast.17, bf16[1024,1024]{1,0:T(8,128)(2,1)} %bitcast.16, bf16[2,512,512]{2,1,0:T(8,128)(2,1)} %pol_hbm.1, f32[512,768]{1,0:T(8,128)} %damp_hbm.1, ...), custom_call_target="tpu_custom_call" | custom-call | tf_op jit(solution)/shard_map/spectral/pallas_call | solution.py:473
  196.2 2.8 %copy.44 = bf16[6,128,2,256]{3,2,1,0:T(2,128)(2,1)} copy(bf16[6,128,2,256]{3,1,2,0:T(8,128)(2,1)} %bitcast.20) | data formatting | bytes 1572864
  199.0 3.8 %copy.46 = bf16[2,1024,768]{2,1,0:T(8,128)(2,1)} copy(bf16[2,1024,768]{2,1,0:T(8,128)(2,1)} %get-tuple-element.14) | data formatting | bytes 6291456
  (7 shorter events, 0.0 us)
Async XLA Ops:
  0.6 14.0 %copy-start = (f32[32,1024]{1,0:T(8,128)S(1)}, f32[32,1024]{1,0:T(8,128)}, u32[]{:S(2)}) copy-start(f32[32,1024]{1,0:T(8,128)} %constant.43.clone) | copy-start | bytes 393220
  0.6 14.0 %copy-start.1 = (f32[32,1024]{1,0:T(8,128)S(1)}, f32[32,1024]{1,0:T(8,128)}, u32[]{:S(2)}) copy-start(f32[32,1024]{1,0:T(8,128)} %constant.42.clone) | copy-start | bytes 393220
  0.7 13.9 %copy-start.2 = (f32[32,1024]{1,0:T(8,128)S(1)}, f32[32,1024]{1,0:T(8,128)}, u32[]{:S(2)}) copy-start(f32[32,1024]{1,0:T(8,128)} %constant.41.clone) | copy-start | bytes 393220
  0.7 13.9 %copy-start.3 = (f32[32,1024]{1,0:T(8,128)S(1)}, f32[32,1024]{1,0:T(8,128)}, u32[]{:S(2)}) copy-start(f32[32,1024]{1,0:T(8,128)} %constant.40.clone) | copy-start | bytes 393220
  8.7 7.9 %copy-start.4 = (s32[128]{0:T(128)}, s32[128]{0:T(128)S(1)}, u32[]{:S(2)}) copy-start(s32[128]{0:T(128)S(1)} %broadcast_in_dim_reshape.2.owner_ref) | copy-start | bytes 1540
  8.9 7.7 %copy-start.5 = (s32[128]{0:T(128)}, s32[128]{0:T(128)S(1)}, u32[]{:S(2)}) copy-start(s32[128]{0:T(128)S(1)} %convert_reduce_fusion.rank_ref) | copy-start | bytes 1540

commit v3 on v2

--- a/solution.py
+++ b/solution.py
@@ -10,40 +10,22 @@
 from jax.sharding import PartitionSpec as P
 
 MESH = pl.DeviceIdType.MESH
-CHUNKS = (256, 256, 256)
+CHUNKS = (128,) * 6
+WINDOW = 3
 NZ, NY, NX, NC = 8, 4, 4, 2
 NP = NY * NX * NC
 N = 1024
 LAT = 512
 
 
-def trig(a, b):
-    phase = (a[:, None].astype(np.int64) * b[None, :]) % N
-    angle = phase.astype(np.float64) * (2.0 * math.pi / N)
-    return np.cos(angle).astype(np.float32), np.sin(angle).astype(np.float32)
-
-
-def basis_tables():
-    n = np.arange(N)
-    zh, zl, part, y = np.meshgrid(np.arange(2), np.arange(4), np.arange(2), np.arange(4), indexing="ij")
-    k_hi = (zl * 128 + y * 32 + zh * 16).reshape(-1)
-    part_hi = part.reshape(-1)[:, None]
-    k_lo = np.arange(16)
-    ch, sh = trig(k_hi, n)
-    cl, sl = trig(k_lo, n)
-    u1 = np.where(part_hi == 0, ch, -sh)
-    u2 = np.where(part_hi == 0, -sh, -ch)
-    fwd = jnp.asarray(u1)[:, None, :] * jnp.asarray(cl)[None] + jnp.asarray(u2)[:, None, :] * jnp.asarray(sl)[None]
-    fwd = fwd.astype(jnp.bfloat16).reshape(N, N)
-    k_all = (k_hi[:, None] + k_lo[None, :]).reshape(-1)
-    part_all = np.repeat(part.reshape(-1), 16)[None, :]
-    c1, s1 = trig(np.arange(32) * 32, k_all)
-    c0, s0 = trig(np.arange(32), k_all)
-    v1 = np.where(part_all == 0, c1, -s1)
-    v2 = np.where(part_all == 0, -s1, -c1)
-    inv = jnp.asarray(v1)[:, None, :] * jnp.asarray(c0)[None] + jnp.asarray(v2)[:, None, :] * jnp.asarray(s0)[None]
-    inv = inv.astype(jnp.bfloat16).reshape(N, N)
-    return fwd, inv
+def basis_table():
+    z_hi, z_lo, part, y, low = np.meshgrid(
+        np.arange(2), np.arange(4), np.arange(2), np.arange(4), np.arange(16), indexing="ij"
+    )
+    k = (z_lo * 128 + y * 32 + z_hi * 16 + low).reshape(-1)[:, None]
+    angle = ((k * np.arange(N)[None, :]) % N).astype(np.float64) * (2.0 * math.pi / N)
+    table = np.where(part.reshape(-1)[:, None] == 0, np.cos(angle), -np.sin(angle))
+    return table.astype(np.float32).astype(jnp.bfloat16)
 
 
 def one_hot(rows, cols, fn):
@@ -63,8 +45,8 @@
 
 
 def spectral_kernel(
-    air_hbm, fwd_hbm, inv_hbm, pol_hbm, damp_hbm, patch_hbm, warm_ref, proj_ref, conv_ref,
-    local_ref, mean_ref, bias_ref, read_ref, wet_ref, total_ref, slot_ref, owner_ref, rank_ref,
+    air_hbm, fwd_hbm, pol_hbm, damp_hbm, patch_hbm, warm_ref, proj_ref, conv_ref,
+    local_ref, mean_ref, bias_ref, read_ref, wet_ref, total_ref, owner_ref,
     out_hbm, ocean_hbm, *scr
 ):
     nchunk = len(CHUNKS)
@@ -80,6 +62,7 @@
     zs2 = [next(it) for _ in CHUNKS]
     fin = [next(it) for _ in CHUNKS]
     patch, x3, q3, q4, fpair, fall, spair, sall, seab, ocean = (next(it) for _ in range(10))
+    conv_t, read_t, local_t, eye, route = (next(it) for _ in range(5))
     load_sem, out_sem, send_sem, recv_sem, self_sem, xs_sem = (next(it) for _ in range(6))
 
     s = lax.axis_index("sec")
@@ -114,7 +97,6 @@
     ld_air = [load(air_hbm.at[:, :, pl.ds(offs[j], CHUNKS[j])], airv[j]) for j in range(nchunk)]
     ld_pol = load(pol_hbm, pol)
     ld_damp = load(damp_hbm, damp)
-    ld_inv = load(inv_hbm, inv)
     ld_patch = load(patch_hbm, patch)
 
     barrier = pltpu.get_barrier_semaphore()
@@ -131,7 +113,8 @@
     lax.fori_loop(1, NP, greet_p, 0)
 
     def z_copy(stage, j, src, dst, i):
-        to = lax.rem(z + i, NZ)
+        near = (i + 1) // 2
+        to = lax.rem(z + jnp.where(lax.rem(i, 2) == 1, near, NZ - near), NZ)
         return pltpu.make_async_remote_copy(
             src_ref=src.at[to], dst_ref=dst.at[z],
             send_sem=send_sem.at[stage, j], recv_sem=recv_sem.at[stage, j],
@@ -238,35 +221,64 @@
         return 0
 
     def ocean_step(i, sea):
-        tile = slot_ref[i]
+        tile = route[i]
         owner_b = tile >> 2
         flux = fall[((owner_b >> 3) << 2) + (owner_b & 3), (owner_b >> 2) & 1, tile & 3].astype(jnp.float32)
         wet = wet_ref[i].astype(jnp.float32)
         masked = [flux[r] * wet[r:r + 1, :] for r in range(2)]
         whole = jnp.sum(masked[0] + masked[1], axis=1, keepdims=True)
         fmean = whole / jnp.maximum(total_ref[i].astype(jnp.float32), 1.0)
-        shift = bias_ref[...]
-        for f in range(8):
-            shift = shift + mean_ref[:, f:f + 1] * fmean[f:f + 1, :]
+        row = jnp.sum(mean_ref[...] * fmean, axis=0, keepdims=True) + bias_ref[...]
+        shift = jnp.broadcast_to(row, (128, 128)).T
+        shift = jnp.concatenate([shift, shift], axis=1)
         for r in range(2):
             wins = [
                 x3[i, r + dr, dw:dw + 256, :].astype(jnp.bfloat16) for dr in range(3) for dw in range(3)
             ]
-            pre = dot_t(conv_ref[...], jnp.concatenate(wins, axis=1))
-            pre = pre + dot(local_ref[...], masked[r].astype(jnp.bfloat16)) + shift
+            pre = dot_t(conv_t[...], jnp.concatenate(wins, axis=1))
+            pre = pre + dot(local_t[...], masked[r].astype(jnp.bfloat16)) + shift
             hidden = jax.nn.gelu(pre, approximate=True).astype(jnp.bfloat16)
-            old = dot_t(read_ref[1], wins[4])
-            new = (old + dot(read_ref[0], hidden)) * wet[r:r + 1, :]
+            old = dot_t(eye[:128, :128], wins[4])
+            new = (old + dot(read_t[...], hidden)) * wet[r:r + 1, :]
             ocean[i, r] = new.astype(jnp.bfloat16)
             line = lax.broadcasted_iota(jnp.int32, (16, 256), 0)
             sea = jnp.where(line == 2 * i + r, jnp.broadcast_to(new[0:1, :], (16, 256)), sea)
         return sea
 
-    def ocean_all():
+    def ocean_prepare():
         q3[...] = one_hot(256, 256, lambda r, q: ((r >> 6) == (q & 3)) & ((r & 63) == (q >> 2)))
         q4[...] = one_hot(32, 256, lambda r, q: q == (r & 7) * 4 + (r >> 3) + 248)
+        small = eye[:128, :128]
+        conv_t[...] = dot_t(small, conv_ref[...]).astype(jnp.bfloat16)
+        read_t[...] = dot_t(small, read_ref[...]).astype(jnp.bfloat16)
+        local_t[...] = dot_t(small, local_ref[...]).astype(jnp.bfloat16)
         ld_patch.wait()
         lax.fori_loop(0, 6, rows_first, 0)
+
+    def find_routes():
+        mine = [owner_ref[q, (s * 32 + b) * 2 + c] for q in range(4)]
+
+        def scan(i, held):
+            held = list(held)
+            for q in range(4):
+                owner = owner_ref[q, (s * 32 + i) * 2 + c]
+                hit = owner == b
+                for k in range(6):
+                    held[k] = jnp.where(hit & (held[6] == k), i * 4 + q, held[k])
+                held[6] = held[6] + jnp.where(hit, 1, 0)
+                for k in range(4):
+                    before = i * 4 + q < b * 4 + k
+                    held[7 + k] = held[7 + k] + jnp.where((owner == mine[k]) & before, 1, 0)
+            return tuple(held)
+
+        held = lax.fori_loop(0, 32, scan, tuple(jnp.int32(0) for _ in range(11)))
+        for k in range(6):
+            route[k] = held[k]
+        for k in range(4):
+            route[8 + k] = mine[k]
+            route[12 + k] = held[7 + k]
+
+    def ocean_all():
         spread_wait(0, fpair, fall)
         sea = lax.fori_loop(0, 6, ocean_step, jnp.zeros((16, 256), jnp.float32))
         spair[z_hi] = sea.astype(jnp.bfloat16)
@@ -276,9 +288,8 @@
     def place_sea():
         spread_wait(1, spair, sall)
         for q in range(4):
-            at = (lax.axis_index("band")) * 4 + q
-            owner = owner_ref[at]
-            slot = rank_ref[at]
+            owner = route[8 + q]
+            slot = route[12 + q]
             tile = sall[((owner >> 3) << 2) + (owner & 3), (owner >> 2) & 1].astype(jnp.float32)
             for t in range(2):
                 line = lax.broadcasted_iota(jnp.int32, (16, 256), 0)
@@ -354,7 +365,7 @@
             old = airv[j][t, pl.ds(m, 256), :].astype(jnp.float32)
             sea = seab[t, pl.ds(m, 256), :]
             sea = jnp.concatenate([sea] * (w // 128), axis=1)
-            new = old + rec + sea * warm_ref[:, d0:d0 + w]
+            new = old + rec + sea * warm_ref[d0:d0 + w][None, :]
             airv[j][t, pl.ds(m, 256), :] = new.astype(jnp.bfloat16)
             return 0
 
@@ -372,6 +383,17 @@
             polt[k] = lax.dot_general(
                 selt, pol[k], (((1,), (1,)), ((), ())), preferred_element_type=jnp.float32
             ).astype(jnp.bfloat16)
+        eye[...] = one_hot(256, 256, lambda r, q: r == q)
+
+        def turn(i, _):
+            r0 = pl.multiple_of((i // 4) * 256, 256)
+            n0 = pl.multiple_of(lax.rem(i, 4) * 256, 256)
+            inv[pl.ds(n0, 256), pl.ds(r0, 256)] = dot_t(
+                eye[...], fwd[pl.ds(r0, 256), pl.ds(n0, 256)]
+            ).astype(jnp.bfloat16)
+            return 0
+
+        lax.fori_loop(0, 16, turn, 0)
         ld_damp.wait()
 
     last = nchunk - 1
@@ -384,16 +406,18 @@
     flip_copy(0, fpair).start()
     for j in range(1, nchunk):
         dft(j)
-        if j == 1:
-            z_start(0, 1, zs1[1], zr1[1])
-    prepare()
+        if j < WINDOW:
+            z_start(0, j, zs1[j], zr1[j])
     flip_copy(0, fpair).wait()
     spread_start(0, fpair, fall)
+    prepare()
+    find_routes()
+    ocean_prepare()
 
     def step_a(j):
         z_wait(0, j, zs1[j], zr1[j])
-        if j + 2 <= last:
-            z_start(0, j + 2, zs1[j + 2], zr1[j + 2])
+        if j + WINDOW <= last:
+            z_start(0, j + WINDOW, zs1[j + WINDOW], zr1[j + WINDOW])
         perm1(j)
         p_start(1, j, ps1[j], mid[j])
 
@@ -409,8 +433,6 @@
 
     def step_d(j):
         z_wait(3, j, zs2[j], fin[j])
-        if j == 0:
-            ld_inv.wait()
         inverse(j)
 
     for i in range(nchunk + 3):
@@ -441,7 +463,7 @@
         pltpu.make_async_copy(airv[j], out_hbm.at[:, :, pl.ds(offs[j], CHUNKS[j])], out_sem.at[j]).wait()
 
 
-def spectral(air, fwd, inv, pol, damp, patch, *rest):
+def spectral(air, fwd, pol, damp, patch, *rest):
     bf = jnp.bfloat16
     n = len(CHUNKS)
     scratch = [
@@ -464,23 +486,25 @@
         pltpu.VMEM((2, 4, 2, 8, 256), bf), pltpu.VMEM((16, 2, 4, 2, 8, 256), bf),
         pltpu.VMEM((2, 16, 256), bf), pltpu.VMEM((16, 2, 16, 256), bf),
         pltpu.VMEM((2, N, 128), jnp.float32), pltpu.VMEM((6, 2, 128, 256), bf),
+        pltpu.VMEM((128, 1152), bf), pltpu.VMEM((128, 128), bf), pltpu.VMEM((128, 8), bf),
+        pltpu.VMEM((256, 256), bf), pltpu.SMEM((16,), jnp.int32),
     ]
     dma = pltpu.SemaphoreType.DMA
-    scratch += [dma((5 + n,)), dma((n,)), dma((4, n)), dma((4, n)), dma((4, n)), dma((2, 6))]
+    scratch += [dma((4 + n,)), dma((n,)), dma((4, n)), dma((4, n)), dma((4, n)), dma((2, 6))]
     anys = pl.BlockSpec(memory_space=pl.ANY)
     vm = pl.BlockSpec(memory_space=pltpu.VMEM)
     sm = pl.BlockSpec(memory_space=pltpu.SMEM)
     return pl.pallas_call(
         spectral_kernel,
         out_shape=(jax.ShapeDtypeStruct(air.shape, bf), jax.ShapeDtypeStruct((6, 2, 128, 256), bf)),
-        in_specs=[anys] * 6 + [vm] * 8 + [sm] * 4,
+        in_specs=[anys] * 5 + [vm] * 8 + [sm] * 2,
         out_specs=(anys, anys),
         scratch_shapes=scratch,
         compiler_params=pltpu.CompilerParams(
             collective_id=0, has_side_effects=True, vmem_limit_bytes=60 << 20
         ),
         name="spectral",
-    )(air, fwd, inv, pol, damp, patch, *rest)
+    )(air, fwd, pol, damp, patch, *rest)
 
 
 def shards(
@@ -499,41 +523,22 @@
     water_point_indicator,
     water_point_totals,
 ):
-    sec_id = lax.axis_index("sec")
-    band_id = lax.axis_index("band")
-    core_id = lax.axis_index("ch")
-    owner_grid = patch_holder_index.reshape(4, 32, 2, 4)
-    owners = lax.dynamic_slice(owner_grid, (sec_id, 0, core_id, 0), (1, 32, 1, 4)).reshape(128)
-    at = jnp.arange(128, dtype=jnp.int32)
-    same = owners[:, None] == owners[None, :]
-    ranks = jnp.sum((same & (at[None, :] < at[:, None])).astype(jnp.int32), axis=1)
-    slot = jnp.arange(6, dtype=jnp.int32)
-    chosen = (owners[None, :] == band_id) & (ranks[None, :] == slot[:, None])
-    slot_tile = jnp.sum(jnp.where(chosen, at[None, :], 0), axis=1)
-    fwd, inv = basis_tables()
-    bf = jnp.bfloat16
-    conv = kernel_coefficients.reshape(9 * 128, 128).T
-    readout = jnp.stack([water_readout_matrix.T, jnp.eye(128, dtype=bf)])
-    patches = water_patch_fields.transpose(0, 3, 2, 1).reshape(6, 1032, 128)
     advanced, ocean = spectral(
         air_field_lattice,
-        fwd,
-        inv,
+        jnp.asarray(basis_table()),
         associated_polynomial_matrix,
         harmonic_damping_factor,
-        patches,
-        warmth_response_factor[None, :],
+        water_patch_fields.transpose(0, 3, 2, 1).reshape(6, 1032, 128),
+        warmth_response_factor,
         boundary_exchange_projector.T,
-        conv,
-        local_exchange_matrix.T,
-        patch_average_matrix.T,
-        water_kernel_offset[:, None],
-        readout,
+        kernel_coefficients.reshape(9 * 128, 128),
+        local_exchange_matrix,
+        patch_average_matrix,
+        water_kernel_offset[None, :],
+        water_readout_matrix,
         water_point_indicator,
         water_point_totals,
-        slot_tile,
-        owners,
-        ranks,
+        patch_holder_index.T,
     )
     return (advanced, ocean.transpose(0, 2, 1, 3))
 

time: 207 us -> 167 us (0.81); the launches traced: 203 us -> 167 us
  Pallas kernels: 180 us -> 160 us
  local copies, waits for them, and re-layouts: 15.8 us -> 6.58 us
  other arithmetic: 6.64 us -> 0 us
    pallas_call x1, Pallas kernels: 180 us -> 160 us  [spectral(): pl.pallas_call(spectral_kernel, out_shape=(jax.ShapeDtypeStruct(air.shape...]
    convert_element_type x3 -> x0, other arithmetic: 5.15 us -> none  [the longest x1 3.13 us: basis_tables(): fwd = fwd.astype(jnp.bfloat16).reshape(N, N)]
    unnamed x18 -> x2, local copies, waits for them, and re-layouts: 11.1 us -> 6.58 us
    broadcast_in_dim x2 -> x0, local copies, waits for them, and re-layouts: 2.74 us -> none  [the longest x1 1.38 us: shards(): water_kernel_offset[:, None]]
where the time goes in v3:
time: 167 us
  Pallas kernels  160 us (96%)
  local copies, waits for them, and re-layouts  6.58 us (4%)
    pallas_call x1, Pallas kernels, spectral(): pl.pallas_call(spectral_kernel, out_shape=(jax.ShapeDtypeStruct(air.shape...  160 us
    unnamed x2, local copies, waits for them, and re-layouts  6.58 us

profile of v3, /device:TPU:1, one launch (start us, length us, event | category | flops | bytes accessed | tf_op | source)
XLA Modules:
  0.0 167.3 jit_solution(7159198476654958936)
XLA Ops:
  0.6 160.1 %spectral.1 = (bf16[2,1024,768]{2,1,0:T(8,128)(2,1)}, bf16[6,2,128,256]{3,2,1,0:T(8,128)(2,1)}) custom-call(bf16[2,1024,768]{2,1,0:T(8,128)(2,1)} %air_hbm.1, bf16[1024,1024]{1,0:T(8,128)(2,1)} %constant.2.clone.fwd_hbm, bf16[2,512,512]{2,1,0:T(8,128)(2,1)} %pol_hbm.1, f32[512,768]{1,0:T(8,128)} %damp_hbm.1, bf16[6,1032,128]{2,1,0:T(8,128)(2,1)} %bitcast.8, ...), custom_call_target="tpu_custom_call" | custom-call | tf_op jit(solution)/shard_map/spectral/pallas_call | solution.py:497
  160.7 2.8 %copy.17 = bf16[6,128,2,256]{3,2,1,0:T(2,128)(2,1)} copy(bf16[6,128,2,256]{3,1,2,0:T(8,128)(2,1)} %bitcast.9) | data formatting | bytes 1572864
  163.5 3.8 %copy.19 = bf16[2,1024,768]{2,1,0:T(8,128)(2,1)} copy(bf16[2,1024,768]{2,1,0:T(8,128)(2,1)} %get-tuple-element.10) | data formatting | bytes 6291456

commit v4 on v3

--- a/solution.py
+++ b/solution.py
@@ -12,6 +12,8 @@
 MESH = pl.DeviceIdType.MESH
 CHUNKS = (128,) * 6
 WINDOW = 3
+LAG = 4
+OCEAN_AT = 1
 NZ, NY, NX, NC = 8, 4, 4, 2
 NP = NY * NX * NC
 N = 1024
@@ -62,7 +64,7 @@
     zs2 = [next(it) for _ in CHUNKS]
     fin = [next(it) for _ in CHUNKS]
     patch, x3, q3, q4, fpair, fall, spair, sall, seab, ocean = (next(it) for _ in range(10))
-    conv_t, read_t, local_t, eye, route = (next(it) for _ in range(5))
+    conv_t, read_t, local_t, eye, q5, route = (next(it) for _ in range(6))
     load_sem, out_sem, send_sem, recv_sem, self_sem, xs_sem = (next(it) for _ in range(6))
 
     s = lax.axis_index("sec")
@@ -231,6 +233,7 @@
         row = jnp.sum(mean_ref[...] * fmean, axis=0, keepdims=True) + bias_ref[...]
         shift = jnp.broadcast_to(row, (128, 128)).T
         shift = jnp.concatenate([shift, shift], axis=1)
+        fresh = []
         for r in range(2):
             wins = [
                 x3[i, r + dr, dw:dw + 256, :].astype(jnp.bfloat16) for dr in range(3) for dw in range(3)
@@ -240,14 +243,17 @@
             hidden = jax.nn.gelu(pre, approximate=True).astype(jnp.bfloat16)
             old = dot_t(eye[:128, :128], wins[4])
             new = (old + dot(read_t[...], hidden)) * wet[r:r + 1, :]
-            ocean[i, r] = new.astype(jnp.bfloat16)
+            fresh.append(new.astype(jnp.bfloat16))
             line = lax.broadcasted_iota(jnp.int32, (16, 256), 0)
             sea = jnp.where(line == 2 * i + r, jnp.broadcast_to(new[0:1, :], (16, 256)), sea)
+        quarters = [fresh[r][:, h * 128:(h + 1) * 128] for h in range(2) for r in range(2)]
+        ocean[i] = dot(q5[...], jnp.concatenate(quarters, axis=0)).astype(jnp.bfloat16)
         return sea
 
     def ocean_prepare():
         q3[...] = one_hot(256, 256, lambda r, q: ((r >> 6) == (q & 3)) & ((r & 63) == (q >> 2)))
         q4[...] = one_hot(32, 256, lambda r, q: q == (r & 7) * 4 + (r >> 3) + 248)
+        q5[...] = one_hot(512, 512, lambda r, q: ((r >> 2) == (q & 127)) & ((r & 3) == (q >> 7)))
         small = eye[:128, :128]
         conv_t[...] = dot_t(small, conv_ref[...]).astype(jnp.bfloat16)
         read_t[...] = dot_t(small, read_ref[...]).astype(jnp.bfloat16)
@@ -296,80 +302,86 @@
                 row = jnp.sum(jnp.where(line == 2 * slot + t, tile, 0.0), axis=0, keepdims=True)
                 seab[t, q * 256:(q + 1) * 256, :] = jnp.broadcast_to(row, (128, 256)).T
 
+    def pair(a, bb):
+        return jnp.concatenate([a, bb], axis=1)
+
     def dft(j):
         w = CHUNKS[j]
 
-        def body(i, _):
-            t = i // 4
-            m = lax.rem(i, 4)
+        def body(m, _):
             rows = fwd[pl.ds(pl.multiple_of(m * 256, 256), 256), :]
-            f = dot(rows, airv[j][t]).astype(jnp.bfloat16)
-            zs1[j][pl.ds(m * 2, 2), t] = f.reshape(2, 128, w)
-            return 0
-
-        lax.fori_loop(0, 8, body, 0)
+            f = dot(rows, pair(airv[j][0], airv[j][1])).astype(jnp.bfloat16)
+            for t in range(2):
+                zs1[j][pl.ds(m * 2, 2), t] = f[:, t * w:(t + 1) * w].reshape(2, 128, w)
+            return 0
+
+        lax.fori_loop(0, 4, body, 0)
 
     def perm1(j):
         w = CHUNKS[j]
 
-        def body(i, _):
-            part = i // 4
-            g = lax.rem(i, 4)
-            r0 = pl.multiple_of(part * 64 + g * 16, 16)
-            xin = zr1[j][:, :, pl.ds(r0, 16), :].reshape(256, w)
+        def body(g, _):
+            r0 = pl.multiple_of(g * 16, 16)
+            xin = pair(
+                zr1[j][:, :, pl.ds(r0, 16), :].reshape(256, w),
+                zr1[j][:, :, pl.ds(r0 + 64, 16), :].reshape(256, w),
+            )
             yo = dot(q1[...], xin).astype(jnp.bfloat16)
-            ps1[j][pl.ds(g * 8, 8), part] = yo.reshape(8, 2, 16, w)
-            return 0
-
-        lax.fori_loop(0, 8, body, 0)
+            for part in range(2):
+                ps1[j][pl.ds(g * 8, 8), part] = yo[:, part * w:(part + 1) * w].reshape(8, 2, 16, w)
+            return 0
+
+        lax.fori_loop(0, 4, body, 0)
 
     def middle(j):
         w = CHUNKS[j]
         d0 = offs[j]
 
-        def body(i, _):
-            part = i // 2
-            k = lax.rem(i, 2)
-            xin = mid[j][part, k].reshape(LAT, w)
+        def body(k, _):
+            xin = pair(mid[j][0, k].reshape(LAT, w), mid[j][1, k].reshape(LAT, w))
             sp = dot(polp[k], xin)
-            sc = (sp * damp[:, d0:d0 + w]).astype(jnp.bfloat16)
+            dm = damp[:, d0:d0 + w]
+            sc = (sp * pair(dm, dm)).astype(jnp.bfloat16)
             fo = dot(polt[k], sc).astype(jnp.bfloat16)
-            ret[j][part, k] = fo.reshape(NP, 16, w)
-            return 0
-
-        lax.fori_loop(0, 4, body, 0)
+            for part in range(2):
+                ret[j][part, k] = fo[:, part * w:(part + 1) * w].reshape(NP, 16, w)
+            return 0
+
+        lax.fori_loop(0, 2, body, 0)
 
     def perm2(j):
         w = CHUNKS[j]
 
-        def body(i, _):
-            part = i // 4
-            g = lax.rem(i, 4)
-            r0 = pl.multiple_of(part * 64 + g * 16, 16)
-            xin = pr2[j][pl.ds(g * 8, 8), part].reshape(256, w)
+        def body(g, _):
+            r0 = pl.multiple_of(g * 16, 16)
+            xin = pair(
+                pr2[j][pl.ds(g * 8, 8), 0].reshape(256, w),
+                pr2[j][pl.ds(g * 8, 8), 1].reshape(256, w),
+            )
             yo = dot(q2[...], xin).astype(jnp.bfloat16)
-            zs2[j][:, :, pl.ds(r0, 16), :] = yo.reshape(8, 2, 16, w)
-            return 0
-
-        lax.fori_loop(0, 8, body, 0)
+            for part in range(2):
+                zs2[j][:, :, pl.ds(r0 + part * 64, 16), :] = yo[:, part * w:(part + 1) * w].reshape(8, 2, 16, w)
+            return 0
+
+        lax.fori_loop(0, 4, body, 0)
 
     def inverse(j):
         w = CHUNKS[j]
         d0 = offs[j]
 
         def body(i, _):
-            t = i // 4
-            m = pl.multiple_of(lax.rem(i, 4) * 256, 256)
+            m = pl.multiple_of(i * 256, 256)
             rows = inv[pl.ds(m, 256), :]
-            rec = dot(rows, fin[j][:, t].reshape(N, w)) * (1.0 / 512.0)
-            old = airv[j][t, pl.ds(m, 256), :].astype(jnp.float32)
-            sea = seab[t, pl.ds(m, 256), :]
-            sea = jnp.concatenate([sea] * (w // 128), axis=1)
-            new = old + rec + sea * warm_ref[d0:d0 + w][None, :]
-            airv[j][t, pl.ds(m, 256), :] = new.astype(jnp.bfloat16)
-            return 0
-
-        lax.fori_loop(0, 8, body, 0)
+            rec = dot(rows, pair(fin[j][:, 0].reshape(N, w), fin[j][:, 1].reshape(N, w))) * (1.0 / 512.0)
+            for t in range(2):
+                old = airv[j][t, pl.ds(m, 256), :].astype(jnp.float32)
+                sea = seab[t, pl.ds(m, 256), :]
+                sea = jnp.concatenate([sea] * (w // 128), axis=1)
+                new = old + rec[:, t * w:(t + 1) * w] + sea * warm_ref[d0:d0 + w][None, :]
+                airv[j][t, pl.ds(m, 256), :] = new.astype(jnp.bfloat16)
+            return 0
+
+        lax.fori_loop(0, 4, body, 0)
         pltpu.make_async_copy(airv[j], out_hbm.at[:, :, pl.ds(d0, w)], out_sem.at[j]).start()
 
     def prepare():
@@ -435,22 +447,22 @@
         z_wait(3, j, zs2[j], fin[j])
         inverse(j)
 
-    for i in range(nchunk + 3):
-        if 0 <= i < nchunk:
+    for i in range(nchunk + LAG):
+        if i < nchunk:
             step_a(i)
-        if i == 0:
+        if i == OCEAN_AT:
             ocean_all()
-        if i == 1:
+        if i == OCEAN_AT + 1:
             flip_copy(1, spair).wait()
             spread_start(1, spair, sall)
-        if i == 3:
-            place_sea()
         if 0 <= i - 1 < nchunk:
             step_b(i - 1)
         if 0 <= i - 2 < nchunk:
             step_c(i - 2)
-        if 0 <= i - 3 < nchunk:
-            step_d(i - 3)
+        if i == LAG:
+            place_sea()
+        if 0 <= i - LAG < nchunk:
+            step_d(i - LAG)
 
     spread_sent(0, fall)
     spread_sent(1, sall)
@@ -485,9 +497,9 @@
         pltpu.VMEM((256, 256), bf), pltpu.VMEM((32, 256), bf),
         pltpu.VMEM((2, 4, 2, 8, 256), bf), pltpu.VMEM((16, 2, 4, 2, 8, 256), bf),
         pltpu.VMEM((2, 16, 256), bf), pltpu.VMEM((16, 2, 16, 256), bf),
-        pltpu.VMEM((2, N, 128), jnp.float32), pltpu.VMEM((6, 2, 128, 256), bf),
+        pltpu.VMEM((2, N, 128), jnp.float32), pltpu.VMEM((6, 512, 128), bf),
         pltpu.VMEM((128, 1152), bf), pltpu.VMEM((128, 128), bf), pltpu.VMEM((128, 8), bf),
-        pltpu.VMEM((256, 256), bf), pltpu.SMEM((16,), jnp.int32),
+        pltpu.VMEM((256, 256), bf), pltpu.VMEM((512, 512), bf), pltpu.SMEM((16,), jnp.int32),
     ]
     dma = pltpu.SemaphoreType.DMA
     scratch += [dma((4 + n,)), dma((n,)), dma((4, n)), dma((4, n)), dma((4, n)), dma((2, 6))]
@@ -496,7 +508,7 @@
     sm = pl.BlockSpec(memory_space=pltpu.SMEM)
     return pl.pallas_call(
         spectral_kernel,
-        out_shape=(jax.ShapeDtypeStruct(air.shape, bf), jax.ShapeDtypeStruct((6, 2, 128, 256), bf)),
+        out_shape=(jax.ShapeDtypeStruct(air.shape, bf), jax.ShapeDtypeStruct((6, 512, 128), bf)),
         in_specs=[anys] * 5 + [vm] * 8 + [sm] * 2,
         out_specs=(anys, anys),
         scratch_shapes=scratch,
@@ -540,7 +552,8 @@
         water_point_totals,
         patch_holder_index.T,
     )
-    return (advanced, ocean.transpose(0, 2, 1, 3))
+    ocean = ocean.reshape(6, 128, 2, 2, 128).transpose(0, 1, 3, 2, 4).reshape(6, 128, 2, 256)
+    return (advanced, ocean)
 
 
 def solution(mesh):

time: 167 us -> 160 us (0.958)
  Pallas kernels: 160 us -> 155 us
  local copies, waits for them, and re-layouts: 6.58 us -> 4.71 us
    pallas_call x1, Pallas kernels: 160 us -> 155 us  [spectral(): pl.pallas_call(spectral_kernel, out_shape=(jax.ShapeDtypeStruct(air.shape...]
    unnamed x2 -> x4, local copies, waits for them, and re-layouts: 6.58 us -> 4.71 us
where the time goes in v4:
time: 160 us
  Pallas kernels  155 us (97%)
  local copies, waits for them, and re-layouts  4.71 us (3%)
    pallas_call x1, Pallas kernels, spectral(): pl.pallas_call(spectral_kernel, out_shape=(jax.ShapeDtypeStruct(air.shape...  155 us
    unnamed x4, local copies, waits for them, and re-layouts  4.71 us

profile of v4, /device:TPU:1, one launch (start us, length us, event | category | flops | bytes accessed | tf_op | source)
XLA Modules:
  0.0 160.0 jit_solution(7971955322553161040)
XLA Ops:
  0.6 154.6 %spectral.1 = (bf16[2,1024,768]{2,1,0:T(8,128)(2,1)}, bf16[6,512,128]{2,1,0:T(8,128)(2,1)}) custom-call(bf16[2,1024,768]{2,1,0:T(8,128)(2,1)} %air_hbm.1, bf16[1024,1024]{1,0:T(8,128)(2,1)} %constant.2.clone.fwd_hbm, bf16[2,512,512]{2,1,0:T(8,128)(2,1)} %pol_hbm.1, f32[512,768]{1,0:T(8,128)} %damp_hbm.1, bf16[6,1032,128]{2,1,0:T(8,128)(2,1)} %bitcast.12, ...), custom_call_target="tpu_custom_call" | custom-call | tf_op jit(solution)/shard_map/spectral/pallas_call | solution.py:509
  155.2 0.0 copy-start
  155.3 3.8 %copy.20 = bf16[2,1024,768]{2,1,0:T(8,128)(2,1)} copy(bf16[2,1024,768]{2,1,0:T(8,128)(2,1)} %get-tuple-element.8) | data formatting | bytes 6291456
  159.1 0.0 copy-done
  159.1 0.9 copy.21
Async XLA Ops:
  155.2 3.8 %copy-start = (bf16[6,512,128]{2,1,0:T(8,128)(2,1)S(1)}, bf16[6,512,128]{2,1,0:T(8,128)(2,1)}, u32[]{:S(2)}) copy-start(bf16[6,512,128]{2,1,0:T(8,128)(2,1)} %get-tuple-element.5) | copy-start | bytes 2359300

commit v5 on v4

--- a/solution.py
+++ b/solution.py
@@ -14,6 +14,9 @@
 WINDOW = 3
 LAG = 4
 OCEAN_AT = 1
+START = 3
+PIECES = 8
+HAND = 1
 NZ, NY, NX, NC = 8, 4, 4, 2
 NP = NY * NX * NC
 N = 1024
@@ -418,7 +421,7 @@
     flip_copy(0, fpair).start()
     for j in range(1, nchunk):
         dft(j)
-        if j < WINDOW:
+        if j < START:
             z_start(0, j, zs1[j], zr1[j])
     flip_copy(0, fpair).wait()
     spread_start(0, fpair, fall)
@@ -428,8 +431,8 @@
 
     def step_a(j):
         z_wait(0, j, zs1[j], zr1[j])
-        if j + WINDOW <= last:
-            z_start(0, j + WINDOW, zs1[j + WINDOW], zr1[j + WINDOW])
+        for e in range(START if j == 0 else j + WINDOW, min(j + WINDOW, last) + 1):
+            z_start(0, e, zs1[e], zr1[e])
         perm1(j)
         p_start(1, j, ps1[j], mid[j])
 
@@ -519,6 +522,40 @@
     )(air, fwd, pol, damp, patch, *rest)
 
 
+def hand_over_kernel(air_in, ocean_in, air_out, ocean_out, air_buf, ocean_buf, in_sems, out_sems):
+    rows = 2 * N // PIECES
+    spots = [(air_in, air_buf, air_out, pl.ds(m * rows, rows)) for m in range(PIECES)]
+    spots += [(ocean_in, ocean_buf, ocean_out, pl.ds(m * 2, 2)) for m in range(3)]
+    reads = [pltpu.make_async_copy(a.at[r], v.at[r], in_sems.at[i]) for i, (a, v, o, r) in enumerate(spots)]
+    writes = [pltpu.make_async_copy(v.at[r], o.at[r], out_sems.at[i]) for i, (a, v, o, r) in enumerate(spots)]
+    for copy in reads:
+        copy.start()
+    for read, write in zip(reads, writes):
+        read.wait()
+        write.start()
+    for copy in writes:
+        copy.wait()
+
+
+def hand_over(air, ocean):
+    anys = pl.BlockSpec(memory_space=pl.ANY)
+    air2, ocean2 = air.reshape(2 * N, -1), ocean
+    a, o = pl.pallas_call(
+        hand_over_kernel,
+        out_shape=tuple(jax.ShapeDtypeStruct(v.shape, v.dtype) for v in (air2, ocean2)),
+        in_specs=[anys] * 2,
+        out_specs=(anys, anys),
+        scratch_shapes=[
+            pltpu.VMEM(air2.shape, air2.dtype), pltpu.VMEM(ocean2.shape, ocean2.dtype),
+            pltpu.SemaphoreType.DMA((PIECES + 3,)), pltpu.SemaphoreType.DMA((PIECES + 3,)),
+        ],
+        compiler_params=pltpu.CompilerParams(vmem_limit_bytes=60 << 20),
+        name="hand_over",
+    )(air2, ocean2)
+    o = o.reshape(6, 128, 2, 2, 128).transpose(0, 1, 3, 2, 4).reshape(6, 128, 2, 256)
+    return a.reshape(air.shape), o
+
+
 def shards(
     air_field_lattice,
     associated_polynomial_matrix,
@@ -552,8 +589,7 @@
         water_point_totals,
         patch_holder_index.T,
     )
-    ocean = ocean.reshape(6, 128, 2, 2, 128).transpose(0, 1, 3, 2, 4).reshape(6, 128, 2, 256)
-    return (advanced, ocean)
+    return hand_over(advanced, ocean)
 
 
 def solution(mesh):

time: 160 us -> 159 us (level)
  local copies, waits for them, and re-layouts: 4.71 us -> 0 us
  Pallas kernels: 155 us -> 158 us
    unnamed x4 -> x0, local copies, waits for them, and re-layouts: 4.71 us -> none
    pallas_call x0 -> x1, Pallas kernels: none -> 3.38 us  [hand_over(): pl.pallas_call(hand_over_kernel, out_shape=tuple((jax.ShapeDtypeStruct(v....]
where the time goes in v5:
time: 159 us
  Pallas kernels  158 us (99%)
    pallas_call x1, Pallas kernels, spectral(): pl.pallas_call(spectral_kernel, out_shape=(jax.ShapeDtypeStruct(air.shape...  155 us
    pallas_call x1, Pallas kernels, hand_over(): pl.pallas_call(hand_over_kernel, out_shape=tuple((jax.ShapeDtypeStruct(v....  3.38 us

profile of v5, /device:TPU:1, one launch (start us, length us, event | category | flops | bytes accessed | tf_op | source)
XLA Modules:
  0.0 158.6 jit_solution(15371946341330573280)
XLA Ops:
  0.6 154.6 %spectral.1 = (bf16[2,1024,768]{2,1,0:T(8,128)(2,1)}, bf16[6,512,128]{2,1,0:T(8,128)(2,1)}) custom-call(bf16[2,1024,768]{2,1,0:T(8,128)(2,1)} %air_hbm.1, bf16[1024,1024]{1,0:T(8,128)(2,1)} %constant.2.clone.fwd_hbm, bf16[2,512,512]{2,1,0:T(8,128)(2,1)} %pol_hbm.1, f32[512,768]{1,0:T(8,128)} %damp_hbm.1, bf16[6,1032,128]{2,1,0:T(8,128)(2,1)} %bitcast.15, ...), custom_call_target="tpu_custom_call" | custom-call | tf_op jit(solution)/shard_map/spectral/pallas_call | solution.py:512
  155.2 3.4 %hand_over.1 = (bf16[2048,768]{1,0:T(8,128)(2,1)}, bf16[6,512,128]{2,1,0:T(8,128)(2,1)}) custom-call(bf16[2048,768]{1,0:T(8,128)(2,1)} %bitcast.14, bf16[6,512,128]{2,1,0:T(8,128)(2,1)} %get-tuple-element.7.ocean_in), custom_call_target="tpu_custom_call" | custom-call | tf_op jit(solution)/shard_map/hand_over/pallas_call | solution.py:543

commit v6 on v5

--- a/solution.py
+++ b/solution.py
@@ -453,15 +453,15 @@
     for i in range(nchunk + LAG):
         if i < nchunk:
             step_a(i)
+        if 0 <= i - 1 < nchunk:
+            step_b(i - 1)
+        if 0 <= i - 2 < nchunk:
+            step_c(i - 2)
         if i == OCEAN_AT:
             ocean_all()
         if i == OCEAN_AT + 1:
             flip_copy(1, spair).wait()
             spread_start(1, spair, sall)
-        if 0 <= i - 1 < nchunk:
-            step_b(i - 1)
-        if 0 <= i - 2 < nchunk:
-            step_c(i - 2)
         if i == LAG:
             place_sea()
         if 0 <= i - LAG < nchunk:

time: 159 us -> 162 us (1.019)
  Pallas kernels: 158 us -> 161 us
    pallas_call x1, Pallas kernels: 155 us -> 157 us  [spectral(): pl.pallas_call(spectral_kernel, out_shape=(jax.ShapeDtypeStruct(air.shape...]
where the time goes in v6:
time: 162 us; the launch traced here: 161 us
  Pallas kernels  161 us (99%)
    pallas_call x1, Pallas kernels, spectral(): pl.pallas_call(spectral_kernel, out_shape=(jax.ShapeDtypeStruct(air.shape...  157 us
    pallas_call x1, Pallas kernels, hand_over(): pl.pallas_call(hand_over_kernel, out_shape=tuple((jax.ShapeDtypeStruct(v....  3.38 us

profile of v6, /device:TPU:1, one launch (start us, length us, event | category | flops | bytes accessed | tf_op | source)
XLA Modules:
  0.0 161.3 jit_solution(462631212200370665)
XLA Ops:
  0.6 157.3 %spectral.1 = (bf16[2,1024,768]{2,1,0:T(8,128)(2,1)}, bf16[6,512,128]{2,1,0:T(8,128)(2,1)}) custom-call(bf16[2,1024,768]{2,1,0:T(8,128)(2,1)} %air_hbm.1, bf16[1024,1024]{1,0:T(8,128)(2,1)} %constant.2.clone.fwd_hbm, bf16[2,512,512]{2,1,0:T(8,128)(2,1)} %pol_hbm.1, f32[512,768]{1,0:T(8,128)} %damp_hbm.1, bf16[6,1032,128]{2,1,0:T(8,128)(2,1)} %bitcast.15, ...), custom_call_target="tpu_custom_call" | custom-call | tf_op jit(solution)/shard_map/spectral/pallas_call | solution.py:512
  157.9 3.4 %hand_over.1 = (bf16[2048,768]{1,0:T(8,128)(2,1)}, bf16[6,512,128]{2,1,0:T(8,128)(2,1)}) custom-call(bf16[2048,768]{1,0:T(8,128)(2,1)} %bitcast.14, bf16[6,512,128]{2,1,0:T(8,128)(2,1)} %get-tuple-element.7.ocean_in), custom_call_target="tpu_custom_call" | custom-call | tf_op jit(solution)/shard_map/hand_over/pallas_call | solution.py:543
